TPU v7x, 32 devices: a whole 2x2x4 slice. The times are simulated.
32 devices in a mesh: frames: 2 (over y), az: 4 (over z), rg: 2 (over x), cplx: 2 (over core).
Axes of the slice: x: 2, y: 2, z: 4, core: 2. Of those that a mesh axis runs over, the one named last changes fastest.
Arguments:
- image: bfloat16 [2048, 2, 1024], P(('frames', 'cplx'), None, ('az', 'rg')), parts along dimension 0, may hold values from -6 to 6
- echoes: bfloat16 [2048, 2, 1024], P(('frames', 'cplx'), None, ('az', 'rg')), parts along dimension 0, may hold values from -6 to 6
- slot_time: int32 [2048], P(('frames', 'az', 'rg')), parts along dimension 0, may hold values from -1 to 1023, as said below
- range_matrix: bfloat16 [2, 1024, 1024], P(None, 'cplx'), may hold values from -0.125 to 0.125
- filter_bank: bfloat16 [16, 2, 512], replicated, may hold values from -0.1875 to 0.1875
- filter_index: int32 [1024], replicated, may hold values from 0 to 15
Outputs:
- gradient: float32 [2048, 2, 1024], P(('frames', 'cplx'), None, ('az', 'rg')), parts along dimension 0
There are 2 independent parts, one for each index of `frames`. A program takes and returns all parts, laid end to end along the dimension named above; an argument that names none is the same for every part. Nothing has to cross between parts.
Inputs may be any that keep to these rules, and one draw needn't show every extreme that they name: `slot_time`: owner o holds slots o * 128 to o * 128 + 127: first the azimuth cells of its echo lines, distinct, increasing and within o * 128 to o * 128 + 127, then -1 in every unused slot. Each owner has at least 64 lines, some owner uses all 128 slots, and the last cell 1024 - 1 always has an echo line.
All inputs are finite; a program needn't handle non-finite values.
Results may differ from a plain program's by a relative error of at most 0.0043.
Values may be sent and summed in bfloat16 or wider, within the bound.
No kernel may reach another device: no remote copies, remote signals or barrier semaphores. Data moves between devices by JAX's collectives and lax.ppermute only.
A program may use at most 192 MiB of HBM per device.

v0:
```python
import functools

import jax
import jax.numpy as jnp
from jax import lax
from jax.experimental import pallas as pl
from jax.experimental.pallas import tpu as pltpu
from jax.sharding import PartitionSpec as P

GROUP = 32
F32 = jnp.float32
BF16 = jnp.bfloat16
VMEM = pl.BlockSpec(memory_space=pltpu.VMEM)
SMEM = pl.BlockSpec(memory_space=pltpu.SMEM)


def mm(a, b):
    return jnp.dot(a, b, preferred_element_type=F32)


def mm_nt(a, b):
    return lax.dot_general(a, b, (((1,), (1,)), ((), ())), preferred_element_type=F32)


def mm_tn(a, b):
    return lax.dot_general(a, b, (((0,), (0,)), ((), ())), preferred_element_type=F32)


def iota(shape, axis):
    return lax.broadcasted_iota(jnp.int32, shape, axis)


def column_of(row):
    size = row.shape[1]
    eye = iota((size, size), 0) == iota((size, size), 1)
    return jnp.sum(jnp.where(eye, jnp.broadcast_to(row, (size, size)), 0.0), axis=1, keepdims=True)


def part_of(count, step):
    return lax.axis_index("rg") ^ step if count == 2 else step


def call(body, out_shape, in_specs, scratch=(), flops=0, out_specs=None, limit=None):
    count = sum(x.size * x.dtype.itemsize for x in jax.tree.leaves(out_shape))
    return pl.pallas_call(
        body,
        out_shape=out_shape,
        in_specs=in_specs,
        out_specs=jax.tree.map(lambda _: VMEM, out_shape) if out_specs is None else out_specs,
        scratch_shapes=list(scratch),
        cost_estimate=pl.CostEstimate(flops=flops, bytes_accessed=count, transcendentals=0),
        compiler_params=pltpu.CompilerParams(vmem_limit_bytes=limit or 20 * 2**20),
    )


def rank_of(ids):
    bins = ids.shape[1]
    key = (ids * bins + iota((1, bins), 1)).astype(F32)
    return jnp.sum((column_of(key) < key).astype(F32), axis=0, keepdims=True)


def split_complex(tmp_ref, values):
    bins = values.shape[0] // 2
    tmp_ref[0 : 2 * bins, :] = values
    return jnp.concatenate(
        [tmp_ref[pl.ds(0, bins, stride=2), :], tmp_ref[pl.ds(1, bins, stride=2), :]], axis=1
    ).astype(BF16)


def times_image(matrix_ref, rows, columns, image):
    cells = image.shape[1] // 2
    from_real = mm(matrix_ref[0, rows, columns], image)
    from_imag = mm(matrix_ref[1, rows, columns], image)
    return jnp.concatenate(
        [from_real[:, :cells] - from_imag[:, cells:], from_real[:, cells:] + from_imag[:, :cells]],
        axis=1,
    )


def half_columns(rows_own, half):
    return pl.ds(pl.multiple_of(half * rows_own, rows_own), rows_own)


def prep_body(parts, bank, cell_count, index_any, time_any, echo_any, image_any, matrix_any, *rest):
    starts_ref, perm_ref, unperm_ref, matrix_ref, moved_ref, begun_ref = rest[:6]
    echo_out = rest[6 : 6 + parts]
    index_ref, time_ref, echo_ref, image_ref, tmp_ref, sems = rest[6 + parts :]
    bins = perm_ref.shape[1]
    rows_own = bins * parts
    rg = lax.axis_index("rg")
    owner = lax.axis_index("az") * parts + rg
    half = lax.axis_index("cplx")
    loads = [
        pltpu.make_async_copy(*pair, sems.at[number])
        for number, pair in enumerate(
            (
                (index_any, index_ref),
                (time_any, time_ref),
                (echo_any, echo_ref),
                (image_any, image_ref),
                (matrix_any, matrix_ref),
                (matrix_any.at[:, :, half_columns(rows_own, 1 - half)], moved_ref),
            )
        )
    ]
    for load in loads:
        load.start()
    loads[0].wait()
    ids_half = index_ref[:, half_columns(rows_own, half)]
    pieces = [ids_half[:, part * bins : (part + 1) * bins] for part in range(parts)]

    def ids_of(part):
        return functools.reduce(
            lambda total, number: jnp.where(part == number, pieces[number], total),
            range(1, parts),
            pieces[0],
        )

    for step in range(parts):
        rank = rank_of(ids_of(part_of(parts, step)))
        perm_ref[step] = (iota((bins, bins), 0).astype(F32) == rank).astype(BF16)
    ids = ids_of(rg)
    unperm_ref[...] = (column_of(rank_of(ids)) == iota((bins, bins), 1).astype(F32)).astype(BF16)
    for number in range(bank + 1):
        starts_ref[number] = jnp.sum((ids < number).astype(F32)).astype(jnp.int32)
    loads[1].wait()
    local = (time_ref[...] - owner * cell_count).astype(F32)
    slots = local.shape[1]
    hits = column_of(local) == iota((slots, cell_count), 1).astype(F32)
    place = hits.astype(BF16)
    occupied = jnp.sum(hits.astype(F32), axis=0, keepdims=True)
    loads[2].wait()
    for step in range(parts):
        part = part_of(parts, step)
        rows = echo_ref[pl.ds(pl.multiple_of(part * 2 * bins, 2 * bins), 2 * bins), :]
        moved = mm(perm_ref[step], split_complex(tmp_ref, mm(rows, place))).astype(BF16)
        echo_out[step][0:bins, :] = moved[:, :cell_count]
        echo_out[step][bins : 2 * bins, :] = moved[:, cell_count:]
        echo_out[step][2 * bins :, :] = jnp.broadcast_to(occupied, (16, cell_count)).astype(BF16)
    loads[3].wait()
    image = split_complex(tmp_ref, image_ref[...].astype(F32))
    loads[4].wait()
    begun_ref[...] = times_image(matrix_ref, slice(None), half_columns(rows_own, half), image)
    loads[5].wait()


def bands_body(seg, bank_ref, fwd_ref, adj_ref):
    bank, _, taps = bank_ref.shape
    count = taps // seg
    later = iota((seg, seg), 1) >= iota((seg, seg), 0)
    zero = jnp.zeros((seg, seg), F32)

    def one(number, carry):
        values = bank_ref[number].astype(F32)
        for part in range(2):
            turned = [zero]
            for block in range(count):
                row = values[part : part + 1, block * seg : (block + 1) * seg]
                turned.append(
                    pltpu.roll(jnp.broadcast_to(row, (seg, seg)), 0, 1, stride=1, stride_axis=0)
                )
            turned.append(zero)
            columns = slice(part * seg, (part + 1) * seg)
            for block in range(count + 1):
                tile = jnp.where(later, turned[block + 1], turned[block]).astype(BF16)
                fwd_ref[number, columns, block * seg : (block + 1) * seg] = tile
                adj_ref[number, (count - block) * seg : (count - block + 1) * seg, columns] = tile
        return carry

    lax.fori_loop(0, bank, one, 0)


def compress_body(parts, image_ref, matrix_ref, perm_ref, begun_ref, *rest):
    outs, tmp_ref = rest[:parts], rest[parts]
    half = lax.axis_index("cplx")
    rows_own, cells = begun_ref.shape[0], begun_ref.shape[1] // 2
    bins = rows_own // parts
    image = split_complex(tmp_ref, image_ref[...].astype(F32))
    for step in range(parts):
        rows = pl.ds(pl.multiple_of(part_of(parts, step) * bins, bins), bins)
        made = begun_ref[rows, :] + times_image(
            matrix_ref, rows, half_columns(rows_own, 1 - half), image
        )
        sent = mm(perm_ref[step], made.astype(BF16)).astype(BF16)
        outs[step][:bins, :] = sent[:, :cells]
        outs[step][bins:, :] = sent[:, cells:]


def fill_blocks(blocks_ref, pieces):
    for ref, at in pieces:
        if len(ref.shape) == 2:
            blocks_ref[at] = ref[...]
        else:
            for number in range(ref.shape[0]):
                blocks_ref[at + number] = ref[number]


def side_bases(parts, halo):
    even = lax.rem(lax.axis_index("az"), 2) == 0
    right = halo + parts
    return jnp.where(even, right, 0), jnp.where(even, 0, right)


def filter_groups(starts_ref, bank, bins, group, work):
    align = min(16, group)
    last = bins - group

    def tile(number, at):
        low, high = starts_ref[number], starts_ref[number + 1]
        first = lax.div(low, align) * align + at * group
        first = pl.multiple_of(jnp.minimum(first, last), align)
        slot = iota((group, 1), 0) + first
        work(number, first, (slot >= low) & (slot < high))

    for number in range(bank):
        tile(number, 0)
    for number in range(bank):
        low, high = starts_ref[number], starts_ref[number + 1]
        count = lax.div(high - lax.div(low, align) * align + (group - 1), group)

        def more(at, carry, number=number):
            tile(number, at)
            return carry

        lax.fori_loop(1, count, more, 0)


def windows(blocks_ref, parts, first, group, bins, span):
    loaded = [
        [blocks_ref[block, pl.ds(side * bins + first, group), :] for block in range(blocks_ref.shape[0])]
        for side in range(2)
    ]
    return jnp.concatenate(
        [
            jnp.concatenate(loaded[side][block : block + span], axis=1)
            for block in range(parts)
            for side in range(2)
        ],
        axis=0,
    )


def forward_body(parts, halo, names, starts_ref, *rest):
    count = len(names)
    pieces, bands_ref = rest[:count], rest[count]
    echoes = rest[count + 1 : -3]
    out_ref, blocks_ref, sum_ref = rest[-3:]
    bank, cells = bands_ref.shape[0], blocks_ref.shape[2]
    bins = blocks_ref.shape[1] // 2
    span = bands_ref.shape[2] // cells
    group = min(GROUP, bins)
    even_base, odd_base = side_bases(parts, halo)
    base = {"even": even_base, "odd": odd_base, "own": halo}
    fill_blocks(blocks_ref, [(ref, base[side] + (part_of(parts, step) if parts == 2 else step)) for ref, (side, step) in zip(pieces, names)])

    def work(number, first, mask):
        made = mm_nt(windows(blocks_ref, parts, first, group, bins, span), bands_ref[number])
        for block in range(parts):
            top = made[2 * block * group : (2 * block + 1) * group]
            low = made[(2 * block + 1) * group : (2 * block + 2) * group]
            for side, value in enumerate((top[:, :cells] - low[:, cells:], top[:, cells:] + low[:, :cells])):
                rows = pl.ds(side * bins + first, group)
                sum_ref[block, rows, :] = jnp.where(mask, value, sum_ref[block, rows, :])

    filter_groups(starts_ref, bank, bins, group, work)
    for step in range(parts):
        part = part_of(parts, step)
        echo = echoes[step][...] if len(echoes) > 1 else echoes[0][step]
        occupied = echo[2 * bins : 2 * bins + 1].astype(F32)
        model = sum_ref[part].astype(BF16).astype(F32)
        out_ref[part] = (occupied * model - echo[: 2 * bins].astype(F32)).astype(BF16)


def adjoint_body(parts, halo, starts_ref, even_ref, own_ref, odd_ref, bands_ref, perm_ref, *rest):
    outs, (blocks_ref, sum_ref) = rest[:parts], rest[parts:]
    bank, cells = bands_ref.shape[0], blocks_ref.shape[2]
    bins = blocks_ref.shape[1] // 2
    span = bands_ref.shape[1] // cells
    group = min(GROUP, bins)
    even_base, odd_base = side_bases(parts, halo)
    fill_blocks(blocks_ref, [(even_ref, even_base), (own_ref, halo), (odd_ref, odd_base)])

    def work(number, first, mask):
        made = mm(windows(blocks_ref, parts, first, group, bins, span), bands_ref[number])
        for block in range(parts):
            top = made[2 * block * group : (2 * block + 1) * group]
            low = made[(2 * block + 1) * group : (2 * block + 2) * group]
            for side, value in enumerate((top[:, :cells] + low[:, cells:], low[:, :cells] - top[:, cells:])):
                rows = pl.ds(side * bins + first, group)
                sum_ref[block, rows, :] = jnp.where(mask, value, sum_ref[block, rows, :])

    filter_groups(starts_ref, bank, bins, group, work)
    for step in range(parts):
        part = part_of(parts, step)
        both = jnp.concatenate([sum_ref[part, :bins, :], sum_ref[part, bins:, :]], axis=1).astype(BF16)
        both = mm(perm_ref[...], both).astype(BF16)
        outs[step][:bins, :] = both[:, :cells]
        outs[step][bins:, :] = both[:, cells:]


def gradient_body(parts, mine, steps, begun, final, *refs):
    pieces, refs = refs[: len(steps)], refs[len(steps) :]
    matrix_ref, refs = refs[0], refs[1:]
    begun_ref, refs = (refs[0], refs[1:]) if begun else (None, refs)
    out_ref = refs[0]
    rows_own = matrix_ref.shape[1]
    cells = pieces[0].shape[-1]
    bins = rows_own // parts
    columns = half_columns(rows_own, lax.axis_index("cplx")) if mine else slice(None)
    total = (begun_ref[0], begun_ref[1]) if begun else None
    for ref, step in zip(pieces, steps):
        for number in range(1 if len(ref.shape) == 2 else ref.shape[0]):
            piece = ref[...] if len(ref.shape) == 2 else ref[number]
            part = part_of(parts, step) if len(ref.shape) == 2 else number
            both = jnp.concatenate([piece[:bins], piece[bins:]], axis=1)
            rows = pl.ds(pl.multiple_of(part * bins, bins), bins)
            made = [mm_tn(both, matrix_ref[side, rows, columns]) for side in range(2)]
            total = made if total is None else [x + y for x, y in zip(total, made)]
    if not final:
        out_ref[0], out_ref[1] = total
        return
    real, imag = total
    out_ref[pl.ds(0, rows_own, stride=2), :] = (real[:cells, :] + imag[cells:, :]).T
    out_ref[pl.ds(1, rows_own, stride=2), :] = (real[cells:, :] - imag[:cells, :]).T


def swap_pairs(count, first):
    pairs = []
    for low in range(first, count - 1, 2):
        pairs += [(low, low + 1), (low + 1, low)]
    return pairs


def on_device(image, echoes, slot_time, range_matrix, filter_bank, filter_index):
    rows_own, _, cells = image.shape
    parts, rows_az = lax.axis_size("rg"), lax.axis_size("az")
    bins = rows_own // parts
    bank, _, taps = filter_bank.shape
    halo = taps // 2 // cells
    span = taps // cells + 1
    flip = [(0, 1), (1, 0)]
    struct = jax.ShapeDtypeStruct
    even_pairs, odd_pairs = swap_pairs(rows_az, 0), swap_pairs(rows_az, 1)

    def halves(x):
        return lax.ppermute(x, "cplx", flip)

    def share(pieces):
        if parts == 2:
            return [pieces[0], lax.ppermute(pieces[1], "rg", flip)]
        return [lax.all_to_all(jnp.stack(pieces), "rg", split_axis=0, concat_axis=0)]

    def sides(x):
        if x.ndim == 3 and x.shape[0] > halo:
            first, last = x[:halo], x[x.shape[0] - halo :]
            is_even = lax.rem(lax.axis_index("az"), 2) == 0
            to_even, to_odd = jnp.where(is_even, last, first), jnp.where(is_even, first, last)
        else:
            to_even = to_odd = x
        even = lax.ppermute(to_even, "az", even_pairs)
        odd = lax.ppermute(to_odd, "az", odd_pairs)
        return even, odd

    image_own = image.reshape(2 * rows_own, cells)
    image_other = halves(image_own)
    piece = struct((2 * bins, cells), BF16)
    starts, perms, unperm, matrix, moved, begun, *echo_pieces = call(
        functools.partial(prep_body, parts, bank, cells),
        (
            struct((bank + 1,), jnp.int32),
            struct((parts, bins, bins), BF16),
            struct((bins, bins), BF16),
            struct(range_matrix.shape, BF16),
            struct((2, rows_own, rows_own), BF16),
            struct((rows_own, 2 * cells), F32),
            *[struct((2 * bins + 16, cells), BF16)] * parts,
        ),
        [pl.BlockSpec(memory_space=pltpu.HBM)] * 5,
        [
            pltpu.VMEM((1, filter_index.shape[0]), jnp.int32),
            pltpu.VMEM((1, slot_time.shape[0]), jnp.int32),
            pltpu.VMEM((2 * rows_own, echoes.shape[2]), BF16),
            pltpu.VMEM((2 * rows_own, cells), BF16),
            pltpu.VMEM((2 * rows_own, cells), F32),
            pltpu.SemaphoreType.DMA((6,)),
        ],
        flops=8 * rows_own * rows_own * cells,
        out_specs=(SMEM, *[VMEM] * (parts + 5)),
    )(
        *[
            pltpu.with_memory_space_constraint(x, pltpu.HBM)
            for x in (
                filter_index.reshape(1, filter_index.shape[0]),
                slot_time.reshape(1, slot_time.shape[0]),
                echoes.reshape(2 * rows_own, echoes.shape[2]),
                image_own,
                range_matrix,
            )
        ]
    )
    compressed = call(
        functools.partial(compress_body, parts),
        [piece] * parts,
        [VMEM] * 4,
        [pltpu.VMEM((2 * rows_own, cells), F32)],
        flops=8 * rows_own * rows_own * cells,
    )(image_other, matrix, perms, begun)
    own = share(compressed)
    pieces, names = [], []
    for step, x in enumerate(own):
        even, odd = sides(x)
        pieces += [x, even, odd]
        names += [("own", step), ("even", step), ("odd", step)]
    echo_own = share(echo_pieces)
    moved = halves(moved)
    forward_bands, adjoint_bands = call(
        functools.partial(bands_body, cells),
        (
            struct((bank, 2 * cells, span * cells), BF16),
            struct((bank, span * cells, 2 * cells), BF16),
        ),
        [VMEM],
        flops=10**9,
    )(filter_bank)
    filter_flops = 2 * bins * parts * 2 * span * cells * 2 * cells
    blocks = pltpu.VMEM((parts + 2 * halo, 2 * bins, cells), BF16)
    sums = pltpu.VMEM((parts, 2 * bins, cells), F32)
    residual = call(
        functools.partial(forward_body, parts, halo, names),
        struct((parts, 2 * bins, cells), BF16),
        [SMEM] + [VMEM] * (len(pieces) + 1 + len(echo_own)),
        [blocks, sums],
        flops=filter_flops,
    )(starts, *pieces, forward_bands, *echo_own)
    even, odd = sides(residual)
    back = call(
        functools.partial(adjoint_body, parts, halo),
        [piece] * parts,
        [SMEM] + [VMEM] * 5,
        [blocks, sums],
        flops=filter_flops,
    )(starts, even, residual, odd, adjoint_bands, unperm)

    def project(pieces, steps, mine, begun=None, final=False):
        out = struct((2 * rows_own, cells), F32) if final else struct((2, 2 * cells, rows_own), F32)
        args = [*pieces, matrix if mine else moved] + ([] if begun is None else [begun])
        return call(
            functools.partial(gradient_body, parts, mine, steps, begun is not None, final),
            out,
            [VMEM] * len(args),
            flops=8 * len(pieces) * rows_own * bins * 2 * cells,
        )(*args)

    back_own = share(back)
    back_other = []
    for x in back_own:
        back_other.append(halves(x))
    total = None
    for number in range(len(back_own)):
        last = number == len(back_own) - 1
        total = project([back_own[number]], [number], True, total)
        total = project([back_other[number]], [number], False, total, last)
    return total.reshape(rows_own, 2, cells)


def solution(mesh):
    return jax.shard_map(
        on_device,
        mesh=mesh,
        in_specs=(
            P(("frames", "cplx"), None, ("az", "rg")),
            P(("frames", "cplx"), None, ("az", "rg")),
            P(("frames", "az", "rg")),
            P(None, "cplx", None),
            P(),
            P(),
        ),
        out_specs=P(("frames", "cplx"), None, ("az", "rg")),
        check_vma=False,
    )
```

profile of v0, /device:TPU:0, one launch (start us, length us, event | category | flops | bytes accessed | tf_op | source)
XLA Modules:
  0.0 43.1 jit_solution(14640827946998800372)
XLA Ops:
  0.0 0.0 copy-start
  0.0 0.5 %collective-permute-start = (bf16[1024,128]{1,0:T(8,128)(2,1)}, bf16[1024,128]{1,0:T(8,128)(2,1)S(1)}, u32[]{:S(2)}, u32[]{:S(2)}) collective-permute-start(bf16[1024,128]{1,0:T(8,128)(2,1)} %bitcast.6), channel_id=1, source_target_pairs={{0,1},{1,0},{2,3},{3,2},{4,5},{5,4},{6,7},{7,6},{8,9},{9,8},{10,11... | collective-permute-start | bytes 786440 | tf_op jit(solution)/shard_map/ppermute | solution.py:346
  0.5 2.9 %shard_map.64 = (s32[17]{0:T(128)S(1)}, bf16[2,256,256]{2,1,0:T(8,128)(2,1)S(1)}, bf16[256,256]{1,0:T(8,128)(2,1)S(1)}, bf16[2,512,1024]{2,1,0:T(8,128)(2,1)S(1)...) custom-call(s32[1,1024]{1,0:T(1,128)} %bitcast.8, ...), custom_call_target="tpu_custom_call" | custom-call | flops 268435456 | bytes 4333636 | tf_op jit(solution)/shard_map/pallas_call | solution.py:367
  3.4 0.1 collective-permute-start.11
  3.5 3.0 %collective-permute-start.6 = (bf16[528,128]{1,0:T(8,128)(2,1)S(1)}, bf16[528,128]{1,0:T(8,128)(2,1)S(1)}, u32[]{:S(2)}, u32[]{:S(2)}) collective-permute-start(bf16[528,128]{1,0:T(8,128)(2,1)S(1)} %get-tuple-element.27), channel_id=1, source_target_pairs={{0,2},{2,0},{1,3},{3,1},{4,6},{6,4},{5,7},{7,5},{8,10},{10,8},{9,1... | collective-permute-start | bytes 405512 | tf_op jit(solution)/shard_map/ppermute | solution.py:350
  6.5 0.0 collective-permute-done.image_ref
  6.5 0.8 %shard_map.65 = (bf16[512,128]{1,0:T(8,128)(2,1)S(1)}, bf16[512,128]{1,0:T(8,128)(2,1)S(1)}) custom-call(bf16[1024,128]{1,0:T(8,128)(2,1)S(1)} %collective-permute-done.image_ref, bf16[2,512,1024]{2,1,0:T(8,128)(2,1)S(1)} %get-tuple-element.20.matrix_ref.refs_1_, bf16[2,256,256]{2,1,0:T(8,128)(2,1)S(1)} %get-tuple-element.21.perm_ref, ...), custom_call_target="tpu_custom_call" | custom-call | flops 268435456 | bytes 262144 | tf_op jit(solution)/shard_map/pallas_call | solution.py:401
  7.3 0.1 collective-permute-start.3
  7.4 0.7 %collective-permute-start.2 = (bf16[512,128]{1,0:T(8,128)(2,1)S(1)}, bf16[512,128]{1,0:T(8,128)(2,1)S(1)}, u32[]{:S(2)}, u32[]{:S(2)}) collective-permute-start(bf16[512,128]{1,0:T(8,128)(2,1)S(1)} %get-tuple-element.23.rest_0_), channel_id=1, source_target_pairs={{4,8},{8,4},{5,9},{9,5},{6,10},{10,6},{7,11},{11,7},{20,24},{24,20... | collective-permute-start | bytes 393224 | tf_op jit(solution)/shard_map/ppermute | solution.py:361
  8.0 5.0 %collective-permute-start.1 = (bf16[512,128]{1,0:T(8,128)(2,1)S(1)}, bf16[512,128]{1,0:T(8,128)(2,1)S(1)}, u32[]{:S(2)}, u32[]{:S(2)}) collective-permute-start(bf16[512,128]{1,0:T(8,128)(2,1)S(1)} %get-tuple-element.23.rest_0_), channel_id=1, source_target_pairs={{0,4},{4,0},{8,12},{12,8},{1,5},{5,1},{9,13},{13,9},{2,6},{6,2},{1... | collective-permute-start | bytes 393224 | tf_op jit(solution)/shard_map/ppermute | solution.py:360
  13.0 0.1 collective-permute-done.3.rest_3_
  13.1 0.7 %collective-permute-start.5 = (bf16[512,128]{1,0:T(8,128)(2,1)S(1)}, bf16[512,128]{1,0:T(8,128)(2,1)S(1)}, u32[]{:S(2)}, u32[]{:S(2)}) collective-permute-start(bf16[512,128]{1,0:T(8,128)(2,1)S(1)} %collective-permute-done.3.rest_3_), channel_id=1, source_target_pairs={{4,8},{8,4},{5,9},{9,5},{6,10},{10,6},{7,11},{11,7},{20,24},{24,20... | collective-permute-start | bytes 393224 | tf_op jit(solution)/shard_map/ppermute | solution.py:361
  13.8 0.0 collective-permute-done.6.rest_8_
  13.8 4.7 %collective-permute-start.4 = (bf16[512,128]{1,0:T(8,128)(2,1)S(1)}, bf16[512,128]{1,0:T(8,128)(2,1)S(1)}, u32[]{:S(2)}, u32[]{:S(2)}) collective-permute-start(bf16[512,128]{1,0:T(8,128)(2,1)S(1)} %collective-permute-done.3.rest_3_), channel_id=1, source_target_pairs={{0,4},{4,0},{8,12},{12,8},{1,5},{5,1},{9,13},{13,9},{2,6},{6,2},{1... | collective-permute-start | bytes 393224 | tf_op jit(solution)/shard_map/ppermute | solution.py:360
  18.5 0.0 copy-done
  18.5 2.5 %shard_map.66 = (bf16[16,256,640]{2,1,0:T(8,128)(2,1)S(1)}, bf16[16,640,256]{2,1,0:T(8,128)(2,1)S(1)}) custom-call(bf16[16,2,512]{2,1,0:T(2,128)(2,1)S(1)} %copy-done), custom_call_target="tpu_custom_call" | custom-call | flops 1000000000 | bytes 10485760 | tf_op jit(solution)/shard_map/pallas_call | solution.py:416
  21.0 0.0 collective-permute-done.2.rest_2_
  21.0 0.0 collective-permute-done.1.rest_1_
  21.0 0.0 collective-permute-done.5.rest_5_
  21.1 0.4 collective-permute-done.4.rest_4_
  21.4 2.9 %shard_map.67.own_ref = bf16[2,512,128]{2,1,0:T(8,128)(2,1)S(1)} custom-call(s32[17]{0:T(128)S(1)} %get-tuple-element.19.starts_ref, bf16[512,128]{1,0:T(8,128)(2,1)S(1)} %get-tuple-element.23.rest_0_, bf16[512,128]{1,0:T(8,128)(2,1)S(1)} %collective-permute-done.1.rest_1_, bf16[512,128]{1,0:T(8,128)(2,1)S(1)} %collective-permute-done.2.rest_2_, ...), custom_call_target="tpu_custom_call" | custom-call | flops 335544320 | bytes 262144 | tf_op jit(solution)/shard_map/pallas_call | solution.py:428
  24.3 0.7 %collective-permute-start.8 = (bf16[2,512,128]{2,1,0:T(8,128)(2,1)S(1)}, bf16[2,512,128]{2,1,0:T(8,128)(2,1)S(1)}, u32[]{:S(2)}, u32[]{:S(2)}) collective-permute-start(bf16[2,512,128]{2,1,0:T(8,128)(2,1)S(1)} %shard_map.67.own_ref), channel_id=1, source_target_pairs={{4,8},{8,4},{5,9},{9,5},{6,10},{10,6},{7,11},{11,7},{20,24},{24,20... | collective-permute-start | bytes 786440 | tf_op jit(solution)/shard_map/ppermute | solution.py:361
  25.0 3.8 %collective-permute-start.7 = (bf16[2,512,128]{2,1,0:T(8,128)(2,1)S(1)}, bf16[2,512,128]{2,1,0:T(8,128)(2,1)S(1)}, u32[]{:S(2)}, u32[]{:S(2)}) collective-permute-start(bf16[2,512,128]{2,1,0:T(8,128)(2,1)S(1)} %shard_map.67.own_ref), channel_id=1, source_target_pairs={{0,4},{4,0},{8,12},{12,8},{1,5},{5,1},{9,13},{13,9},{2,6},{6,2},{1... | collective-permute-start | bytes 786440 | tf_op jit(solution)/shard_map/ppermute | solution.py:360
  28.8 0.0 collective-permute-done.8.odd_ref
  28.8 4.4 %collective-permute-done.7.even_ref = bf16[2,512,128]{2,1,0:T(8,128)(2,1)S(1)} collective-permute-done((bf16[2,512,128]{2,1,0:T(8,128)(2,1)S(1)}, bf16[2,512,128]{2,1,0:T(8,128)(2,1)S(1)}, u32[]{:S(2)}, u32[]{:S(2)}) %collective-permute-start.7) | collective-permute-done | bytes 262176 | tf_op jit(solution)/shard_map/ppermute | solution.py:360
  33.2 2.3 %shard_map.68 = (bf16[512,128]{1,0:T(8,128)(2,1)S(1)}, bf16[512,128]{1,0:T(8,128)(2,1)S(1)}) custom-call(s32[17]{0:T(128)S(1)} %get-tuple-element.19.starts_ref, bf16[2,512,128]{2,1,0:T(8,128)(2,1)S(1)} %collective-permute-done.7.even_ref, bf16[2,512,128]{2,1,0:T(8,128)(2,1)S(1)} %shard_map.67.own_ref, ...), custom_call_target="tpu_custom_call" | custom-call | flops 335544320 | bytes 262144 | tf_op jit(solution)/shard_map/pallas_call | solution.py:436
  35.5 2.0 %collective-permute-start.9 = (bf16[512,128]{1,0:T(8,128)(2,1)S(1)}, bf16[512,128]{1,0:T(8,128)(2,1)S(1)}, u32[]{:S(2)}, u32[]{:S(2)}) collective-permute-start(bf16[512,128]{1,0:T(8,128)(2,1)S(1)} %get-tuple-element.30), channel_id=1, source_target_pairs={{0,2},{2,0},{1,3},{3,1},{4,6},{6,4},{5,7},{7,5},{8,10},{10,8},{9,1... | collective-permute-start | bytes 393224 | tf_op jit(solution)/shard_map/ppermute | solution.py:350
  37.5 0.0 collective-permute-start.12
  37.5 3.1 %collective-permute-done.9.refs_0_ = bf16[512,128]{1,0:T(8,128)(2,1)S(1)} collective-permute-done((bf16[512,128]{1,0:T(8,128)(2,1)S(1)}, bf16[512,128]{1,0:T(8,128)(2,1)S(1)}, u32[]{:S(2)}, u32[]{:S(2)}) %collective-permute-start.9) | collective-permute-done | bytes 131104 | tf_op jit(solution)/shard_map/ppermute | solution.py:350
  40.5 0.0 collective-permute-start.10
  40.5 0.3 shard_map.69.refs_2_
  40.9 0.0 collective-permute-done.12.refs_0_
  40.9 0.0 collective-permute-done.11.refs_1_
  40.9 0.3 shard_map.70.refs_2_
  41.2 0.3 shard_map.71.refs_2_
  41.5 0.4 collective-permute-done.10.refs_0_
  41.9 1.3 %shard_map.72 = f32[1024,128]{1,0:T(8,128)} custom-call(bf16[512,128]{1,0:T(8,128)(2,1)S(1)} %collective-permute-done.10.refs_0_, bf16[2,512,512]{2,1,0:T(8,128)(2,1)S(1)} %collective-permute-done.11.refs_1_, f32[2,256,512]{2,1,0:T(8,128)S(1)} %shard_map.71.refs_2_), custom_call_target="tpu_custom_call" | custom-call | flops 268435456 | bytes 524288 | tf_op jit(solution)/shard_map/pallas_call | solution.py:447
Async XLA Ops:
  0.0 18.5 %copy-start = (bf16[16,2,512]{2,1,0:T(2,128)(2,1)S(1)}, bf16[16,2,512]{2,1,0:T(2,128)(2,1)}, u32[]{:S(2)}) copy-start(bf16[16,2,512]{2,1,0:T(2,128)(2,1)} %bank_ref.1) | copy-start | bytes 98308
  0.0 6.5 %collective-permute-start = (bf16[1024,128]{1,0:T(8,128)(2,1)}, bf16[1024,128]{1,0:T(8,128)(2,1)S(1)}, u32[]{:S(2)}, u32[]{:S(2)}) collective-permute-start(bf16[1024,128]{1,0:T(8,128)(2,1)} %bitcast.6), channel_id=1, source_target_pairs={{0,1},{1,0},{2,3},{3,2},{4,5},{5,4},{6,7},{7,6},{8,9},{9,8},{10,11... | collective-permute-start | bytes 786440 | tf_op jit(solution)/shard_map/ppermute | solution.py:346
  3.4 37.5 %collective-permute-start.11 = (bf16[2,512,512]{2,1,0:T(8,128)(2,1)S(1)}, bf16[2,512,512]{2,1,0:T(8,128)(2,1)S(1)}, u32[]{:S(2)}, u32[]{:S(2)}) collective-permute-start(bf16[2,512,512]{2,1,0:T(8,128)(2,1)S(1)} %get-tuple-element.31), channel_id=1, source_target_pairs={{0,1},{1,0},{2,3},{3,2},{4,5},{5,4},{6,7},{7,6},{8,9},{9,8},{10,11... | collective-permute-start | bytes 3145736 | tf_op jit(solution)/shard_map/ppermute | solution.py:346
  3.5 10.3 %collective-permute-start.6 = (bf16[528,128]{1,0:T(8,128)(2,1)S(1)}, bf16[528,128]{1,0:T(8,128)(2,1)S(1)}, u32[]{:S(2)}, u32[]{:S(2)}) collective-permute-start(bf16[528,128]{1,0:T(8,128)(2,1)S(1)} %get-tuple-element.27), channel_id=1, source_target_pairs={{0,2},{2,0},{1,3},{3,1},{4,6},{6,4},{5,7},{7,5},{8,10},{10,8},{9,1... | collective-permute-start | bytes 405512 | tf_op jit(solution)/shard_map/ppermute | solution.py:350
  7.3 5.8 %collective-permute-start.3 = (bf16[512,128]{1,0:T(8,128)(2,1)S(1)}, bf16[512,128]{1,0:T(8,128)(2,1)S(1)}, u32[]{:S(2)}, u32[]{:S(2)}) collective-permute-start(bf16[512,128]{1,0:T(8,128)(2,1)S(1)} %get-tuple-element.24), channel_id=1, source_target_pairs={{0,2},{2,0},{1,3},{3,1},{4,6},{6,4},{5,7},{7,5},{8,10},{10,8},{9,1... | collective-permute-start | bytes 393224 | tf_op jit(solution)/shard_map/ppermute | solution.py:350
  7.4 13.7 %collective-permute-start.2 = (bf16[512,128]{1,0:T(8,128)(2,1)S(1)}, bf16[512,128]{1,0:T(8,128)(2,1)S(1)}, u32[]{:S(2)}, u32[]{:S(2)}) collective-permute-start(bf16[512,128]{1,0:T(8,128)(2,1)S(1)} %get-tuple-element.23.rest_0_), channel_id=1, source_target_pairs={{4,8},{8,4},{5,9},{9,5},{6,10},{10,6},{7,11},{11,7},{20,24},{24,20... | collective-permute-start | bytes 393224 | tf_op jit(solution)/shard_map/ppermute | solution.py:361
  8.0 13.0 %collective-permute-start.1 = (bf16[512,128]{1,0:T(8,128)(2,1)S(1)}, bf16[512,128]{1,0:T(8,128)(2,1)S(1)}, u32[]{:S(2)}, u32[]{:S(2)}) collective-permute-start(bf16[512,128]{1,0:T(8,128)(2,1)S(1)} %get-tuple-element.23.rest_0_), channel_id=1, source_target_pairs={{0,4},{4,0},{8,12},{12,8},{1,5},{5,1},{9,13},{13,9},{2,6},{6,2},{1... | collective-permute-start | bytes 393224 | tf_op jit(solution)/shard_map/ppermute | solution.py:360
  13.1 8.0 %collective-permute-start.5 = (bf16[512,128]{1,0:T(8,128)(2,1)S(1)}, bf16[512,128]{1,0:T(8,128)(2,1)S(1)}, u32[]{:S(2)}, u32[]{:S(2)}) collective-permute-start(bf16[512,128]{1,0:T(8,128)(2,1)S(1)} %collective-permute-done.3.rest_3_), channel_id=1, source_target_pairs={{4,8},{8,4},{5,9},{9,5},{6,10},{10,6},{7,11},{11,7},{20,24},{24,20... | collective-permute-start | bytes 393224 | tf_op jit(solution)/shard_map/ppermute | solution.py:361
  13.8 7.6 %collective-permute-start.4 = (bf16[512,128]{1,0:T(8,128)(2,1)S(1)}, bf16[512,128]{1,0:T(8,128)(2,1)S(1)}, u32[]{:S(2)}, u32[]{:S(2)}) collective-permute-start(bf16[512,128]{1,0:T(8,128)(2,1)S(1)} %collective-permute-done.3.rest_3_), channel_id=1, source_target_pairs={{0,4},{4,0},{8,12},{12,8},{1,5},{5,1},{9,13},{13,9},{2,6},{6,2},{1... | collective-permute-start | bytes 393224 | tf_op jit(solution)/shard_map/ppermute | solution.py:360
  24.3 4.5 %collective-permute-start.8 = (bf16[2,512,128]{2,1,0:T(8,128)(2,1)S(1)}, bf16[2,512,128]{2,1,0:T(8,128)(2,1)S(1)}, u32[]{:S(2)}, u32[]{:S(2)}) collective-permute-start(bf16[2,512,128]{2,1,0:T(8,128)(2,1)S(1)} %shard_map.67.own_ref), channel_id=1, source_target_pairs={{4,8},{8,4},{5,9},{9,5},{6,10},{10,6},{7,11},{11,7},{20,24},{24,20... | collective-permute-start | bytes 786440 | tf_op jit(solution)/shard_map/ppermute | solution.py:361
  25.0 8.1 %collective-permute-start.7 = (bf16[2,512,128]{2,1,0:T(8,128)(2,1)S(1)}, bf16[2,512,128]{2,1,0:T(8,128)(2,1)S(1)}, u32[]{:S(2)}, u32[]{:S(2)}) collective-permute-start(bf16[2,512,128]{2,1,0:T(8,128)(2,1)S(1)} %shard_map.67.own_ref), channel_id=1, source_target_pairs={{0,4},{4,0},{8,12},{12,8},{1,5},{5,1},{9,13},{13,9},{2,6},{6,2},{1... | collective-permute-start | bytes 786440 | tf_op jit(solution)/shard_map/ppermute | solution.py:360
  35.5 5.0 %collective-permute-start.9 = (bf16[512,128]{1,0:T(8,128)(2,1)S(1)}, bf16[512,128]{1,0:T(8,128)(2,1)S(1)}, u32[]{:S(2)}, u32[]{:S(2)}) collective-permute-start(bf16[512,128]{1,0:T(8,128)(2,1)S(1)} %get-tuple-element.30), channel_id=1, source_target_pairs={{0,2},{2,0},{1,3},{3,1},{4,6},{6,4},{5,7},{7,5},{8,10},{10,8},{9,1... | collective-permute-start | bytes 393224 | tf_op jit(solution)/shard_map/ppermute | solution.py:350
  37.5 3.4 %collective-permute-start.12 = (bf16[512,128]{1,0:T(8,128)(2,1)S(1)}, bf16[512,128]{1,0:T(8,128)(2,1)S(1)}, u32[]{:S(2)}, u32[]{:S(2)}) collective-permute-start(bf16[512,128]{1,0:T(8,128)(2,1)S(1)} %get-tuple-element.32.refs_0_), channel_id=1, source_target_pairs={{0,1},{1,0},{2,3},{3,2},{4,5},{5,4},{6,7},{7,6},{8,9},{9,8},{10,11... | collective-permute-start | bytes 393224 | tf_op jit(solution)/shard_map/ppermute | solution.py:346
  40.5 1.3 %collective-permute-start.10 = (bf16[512,128]{1,0:T(8,128)(2,1)S(1)}, bf16[512,128]{1,0:T(8,128)(2,1)S(1)}, u32[]{:S(2)}, u32[]{:S(2)}) collective-permute-start(bf16[512,128]{1,0:T(8,128)(2,1)S(1)} %collective-permute-done.9.refs_0_), channel_id=1, source_target_pairs={{0,1},{1,0},{2,3},{3,2},{4,5},{5,4},{6,7},{7,6},{8,9},{9,8},{10,11... | collective-permute-start | bytes 393224 | tf_op jit(solution)/shard_map/ppermute | solution.py:346
where the time goes:
time: 43.3 us; the launch traced here: 43.1 us
  starting transfers between devices  21 us (48%)
  Pallas kernels  13.7 us (32%)
  waiting for transfers between devices  8.26 us (19%)
    ppermute x3, starting transfers between devices, sides(): even = lax.ppermute(to_even, 'az', even_pairs)  13.4 us
    ppermute x3, starting transfers between devices, share(): return [pieces[0], lax.ppermute(pieces[1], 'rg', flip)]  5 us
    ppermute x3, waiting for transfers between devices, sides(): even = lax.ppermute(to_even, 'az', even_pairs)  4.74 us
    ppermute x3, waiting for transfers between devices, share(): return [pieces[0], lax.ppermute(pieces[1], 'rg', flip)]  3.15 us
    pallas_call x1, Pallas kernels, on_device(): call(functools.partial(forward_body, parts, halo, names), struct((parts,...  2.93 us
    pallas_call x1, Pallas kernels, on_device(): call(functools.partial(prep_body, parts, bank, cells), (struct((bank + 1,...  2.89 us
    pallas_call x1, Pallas kernels, on_device(): call(functools.partial(bands_body, cells), (struct((bank, 2 * cells, span...  2.55 us
    pallas_call x1, Pallas kernels, on_device(): call(functools.partial(adjoint_body, parts, halo), [piece] * parts, [SMEM...  2.32 us
  transfers between devices with their start and end apart: 13, of which 5 were waited for; matrix products, arithmetic and copies ran while one was open for 0% of the time, Pallas kernels for 29%

commit v1 on v0

v1 whole, which is shorter than its diff:
```python
import functools

import jax
import jax.numpy as jnp
from jax import lax
from jax.experimental import pallas as pl
from jax.experimental.pallas import tpu as pltpu
from jax.sharding import PartitionSpec as P

GROUP = 48
ALIGN = 16
UNROLL = 3
F32 = jnp.float32
BF16 = jnp.bfloat16
VMEM = pl.BlockSpec(memory_space=pltpu.VMEM)
SMEM = pl.BlockSpec(memory_space=pltpu.SMEM)


def mm(a, b):
    return jnp.dot(a, b, preferred_element_type=F32)


def iota(shape, axis):
    return lax.broadcasted_iota(jnp.int32, shape, axis)


def column_of(row):
    size = row.shape[1]
    eye = iota((size, size), 0) == iota((size, size), 1)
    return jnp.sum(jnp.where(eye, jnp.broadcast_to(row, (size, size)), 0.0), axis=1, keepdims=True)


def part_of(count, step):
    return lax.axis_index("rg") ^ step if count == 2 else step


def call(body, out_shape, in_specs, scratch=(), flops=0, out_specs=None, limit=None):
    count = sum(x.size * x.dtype.itemsize for x in jax.tree.leaves(out_shape))
    return pl.pallas_call(
        body,
        out_shape=out_shape,
        in_specs=in_specs,
        out_specs=jax.tree.map(lambda _: VMEM, out_shape) if out_specs is None else out_specs,
        scratch_shapes=list(scratch),
        cost_estimate=pl.CostEstimate(flops=flops, bytes_accessed=count, transcendentals=0),
        compiler_params=pltpu.CompilerParams(vmem_limit_bytes=limit or 20 * 2**20),
    )


def rank_of(ids):
    bins = ids.shape[1]
    key = (ids * bins + iota((1, bins), 1)).astype(F32)
    return jnp.sum((column_of(key) < key).astype(F32), axis=0, keepdims=True)


def split_complex(tmp_ref, values):
    bins = values.shape[0] // 2
    tmp_ref[0 : 2 * bins, :] = values
    return jnp.concatenate(
        [tmp_ref[pl.ds(0, bins, stride=2), :], tmp_ref[pl.ds(1, bins, stride=2), :]], axis=1
    ).astype(BF16)


def times_image(matrix_ref, rows, columns, image):
    cells = image.shape[1] // 2
    from_real = mm(matrix_ref[0, rows, columns], image)
    from_imag = mm(matrix_ref[1, rows, columns], image)
    return jnp.concatenate(
        [from_real[:, :cells] - from_imag[:, cells:], from_real[:, cells:] + from_imag[:, :cells]],
        axis=1,
    )


def half_columns(rows_own, half):
    return pl.ds(pl.multiple_of(half * rows_own, rows_own), rows_own)


def prep_body(parts, index_any, image_any, matrix_any, *rest):
    perm_ref, matrix_ref, begun_ref, index_ref, image_ref, tmp_ref, sems = rest
    bins, rows_own = perm_ref.shape[1:]
    half = lax.axis_index("cplx")
    loads = [
        pltpu.make_async_copy(*pair, sems.at[number])
        for number, pair in enumerate(
            ((index_any, index_ref), (image_any, image_ref), (matrix_any, matrix_ref))
        )
    ]
    for load in loads:
        load.start()
    loads[0].wait()
    rank = rank_of(index_ref[:, half_columns(rows_own, half)])
    for step in range(parts):
        slot = (iota((bins, 1), 0) + part_of(parts, step) * bins).astype(F32)
        perm_ref[step] = (slot == rank).astype(BF16)
    loads[1].wait()
    image = split_complex(tmp_ref, image_ref[...].astype(F32))
    loads[2].wait()
    begun_ref[...] = times_image(matrix_ref, slice(None), half_columns(rows_own, half), image)


def make_bands(seg, starts_ref, table_ref, bands_ref):
    count = table_ref.shape[1] // seg
    later = iota((seg, seg), 1) >= iota((seg, seg), 0)

    def one(number):
        for part in range(2):
            row = table_ref[pl.ds(2 * number + part, 1), :]
            before = jnp.zeros((seg, seg), F32)
            columns = slice(part * seg, (part + 1) * seg)
            for block in range(count):
                same = jnp.broadcast_to(row[:, block * seg : (block + 1) * seg], (seg, seg))
                turned = pltpu.roll(same, 0, 1, stride=1, stride_axis=0)
                tile = jnp.where(later, turned, before).astype(BF16)
                bands_ref[number, (count - 1 - block) * seg : (count - block) * seg, columns] = tile
                before = turned

    def one_used(number, carry):
        pl.when(starts_ref[number + 1] > starts_ref[number])(lambda: one(number))
        return carry

    lax.fori_loop(0, bands_ref.shape[0], one_used, 0)


def fill_table(bank_ref, table_ref):
    bank, _, taps = bank_ref.shape
    table_ref[:, taps:] = jnp.zeros((2 * bank, table_ref.shape[1] - taps), F32)
    for number in range(bank):
        table_ref[2 * number : 2 * number + 2, :taps] = bank_ref[number].astype(F32)


def adjoint_bands_body(seg, starts_ref, bank_ref, bands_ref, table_ref):
    fill_table(bank_ref, table_ref)
    make_bands(seg, starts_ref, table_ref, bands_ref)


def list_tiles(ids, group, starts_ref, number_ref, first_ref):
    bank, bins = starts_ref.shape[0] - 2, ids.shape[1] // lax.axis_size("rg")
    base = lax.axis_index("rg") * bins
    for number in range(bank + 1):
        before = jnp.sum((ids < number).astype(F32)).astype(jnp.int32)
        starts_ref[number] = jnp.clip(before - base, 0, bins)

    def per_filter(number, count):
        low, high = starts_ref[number], starts_ref[number + 1]
        aligned = lax.div(low, ALIGN) * ALIGN

        def per_tile(at, count):
            number_ref[count] = number
            first_ref[count] = jnp.minimum(aligned + at * group, bins - group)
            return count + 1

        tiles = jnp.where(high > low, lax.div(high - aligned + (group - 1), group), 0)
        return lax.fori_loop(0, tiles, per_tile, count)

    count = lax.fori_loop(0, bank, per_filter, 0)
    starts_ref[bank + 1] = count
    for extra in range(UNROLL - 1):
        number_ref[count + extra] = number_ref[count - 1]
        first_ref[count + extra] = first_ref[count - 1]


def bands_body(cell_count, group, index_ref, bank_ref, *rest):
    starts_ref, number_ref, first_ref, bands_ref, table_ref = rest
    _, _, taps = bank_ref.shape
    rows_own = index_ref.shape[1] // lax.axis_size("cplx")
    ids = index_ref[:, half_columns(rows_own, lax.axis_index("cplx"))]
    list_tiles(ids, group, starts_ref, number_ref, first_ref)
    fill_table(bank_ref, table_ref)
    width = table_ref.shape[1]
    turn = (iota((taps, width), 0) + iota((taps, width), 1) == taps).astype(BF16)
    table_ref[...] = mm(table_ref[:, :taps].astype(BF16), turn)
    make_bands(cell_count, starts_ref, table_ref, bands_ref)


def echo_body(parts, cell_count, time_any, echo_any, perm_ref, *rest):
    outs, (time_ref, echo_ref, tmp_ref, sems) = rest[:parts], rest[parts:]
    bins = perm_ref.shape[1]
    owner = lax.axis_index("az") * parts + lax.axis_index("rg")
    loads = [
        pltpu.make_async_copy(time_any, time_ref, sems.at[0]),
        pltpu.make_async_copy(echo_any, echo_ref, sems.at[1]),
    ]
    for load in loads:
        load.start()
    loads[0].wait()
    local = (time_ref[...] - owner * cell_count).astype(F32)
    slots = local.shape[1]
    hits = column_of(local) == iota((slots, cell_count), 1).astype(F32)
    place = hits.astype(BF16)
    occupied = jnp.sum(hits.astype(F32), axis=0, keepdims=True)
    loads[1].wait()
    gridded = split_complex(tmp_ref, mm(echo_ref[...], place))
    for step in range(parts):
        moved = mm(perm_ref[step], gridded).astype(BF16)
        outs[step][0:bins, :] = moved[:, :cell_count]
        outs[step][bins : 2 * bins, :] = moved[:, cell_count:]
        outs[step][2 * bins :, :] = jnp.broadcast_to(occupied, (16, cell_count)).astype(BF16)


def compress_body(step, image_ref, matrix_ref, perm_ref, begun_ref, out_ref, made_ref, tmp_ref):
    rows_own = begun_ref.shape[0]
    image = split_complex(tmp_ref, image_ref[...].astype(F32))
    columns = half_columns(rows_own, 1 - lax.axis_index("cplx"))
    made_ref[...] = (begun_ref[...] + times_image(matrix_ref, slice(None), columns, image)).astype(BF16)
    sort_body(step, made_ref, perm_ref, out_ref)


def sort_body(step, made_ref, perm_ref, out_ref):
    bins, cells = perm_ref.shape[1], made_ref.shape[1] // 2
    sent = mm(perm_ref[step], made_ref[...]).astype(BF16)
    out_ref[:bins, :] = sent[:, :cells]
    out_ref[bins:, :] = sent[:, cells:]


def sorted_matrix(parts, matrix_ref, perm_ref, columns, store):
    bins = perm_ref.shape[1]
    for step in range(parts):
        rows = pl.ds(pl.multiple_of(part_of(parts, step) * bins, bins), bins)
        for side in range(2):
            store(side, rows, mm(perm_ref[step], matrix_ref[side, :, columns]).astype(BF16))


def sort_sent_body(parts, matrix_ref, perm_ref, out_ref):
    def store(side, rows, value):
        out_ref[side, rows, :] = value

    columns = half_columns(matrix_ref.shape[1], 1 - lax.axis_index("cplx"))
    sorted_matrix(parts, matrix_ref, perm_ref, columns, store)


def fill_blocks(blocks_ref, pieces):
    for ref, at in pieces:
        if len(ref.shape) == 2:
            blocks_ref[at] = ref[...]
        else:
            for number in range(ref.shape[0]):
                blocks_ref[at + number] = ref[number]


def side_bases(parts, halo):
    even = lax.rem(lax.axis_index("az"), 2) == 0
    right = halo + parts
    return jnp.where(even, right, 0), jnp.where(even, 0, right)


def filter_groups(starts_ref, number_ref, first_ref, group, work):
    def run(chunk, carry):
        for at in range(UNROLL):
            number = number_ref[chunk * UNROLL + at]
            first = pl.multiple_of(first_ref[chunk * UNROLL + at], ALIGN)
            slot = iota((group, 1), 0) + first
            work(number, first, (slot >= starts_ref[number]) & (slot < starts_ref[number + 1]))
        return carry

    count = starts_ref[starts_ref.shape[0] - 1]
    lax.fori_loop(0, lax.div(count + (UNROLL - 1), UNROLL), run, 0)


def filtered(blocks_ref, bands, outputs, first, group, sign):
    cells, bins = blocks_ref.shape[2], blocks_ref.shape[1] // 2
    span = bands.shape[0] // cells
    rows = [
        jnp.concatenate(
            [blocks_ref[block + at, pl.ds(side * bins + first, group), :] for at in range(span)], axis=1
        )
        for block in outputs
        for side in range(2)
    ]
    made = mm(jnp.concatenate(rows, axis=0), bands)
    results = []
    for number in range(len(outputs)):
        top = made[2 * number * group : (2 * number + 1) * group]
        low = made[(2 * number + 1) * group : (2 * number + 2) * group]
        results.append(
            (top[:, :cells] - sign * low[:, cells:], low[:, :cells] + sign * top[:, cells:])
        )
    return results


def filter_all(parts, group, tiles, blocks_ref, bands_ref, sum_ref, sign):
    bins = blocks_ref.shape[1] // 2

    def work(number, first, mask):
        made = filtered(blocks_ref, bands_ref[number], range(parts), first, group, sign)
        for block in range(parts):
            for side in range(2):
                rows = pl.ds(side * bins + first, group)
                sum_ref[block, rows, :] = jnp.where(mask, made[block][side], sum_ref[block, rows, :])

    filter_groups(*tiles, group, work)


def forward_body(parts, halo, group, names, *refs):
    tiles, rest = refs[:3], refs[3:]
    count = len(names)
    pieces, bands_ref = rest[:count], rest[count]
    echoes = rest[count + 1 : -3]
    out_ref, blocks_ref, sum_ref = rest[-3:]
    bins = blocks_ref.shape[1] // 2
    even_base, odd_base = side_bases(parts, halo)
    base = {"even": even_base, "odd": odd_base, "own": halo}
    fill_blocks(
        blocks_ref,
        [
            (ref, base[side] + (part_of(parts, step) if parts == 2 else step))
            for ref, (side, step) in zip(pieces, names)
        ],
    )
    filter_all(parts, group, tiles, blocks_ref, bands_ref, sum_ref, 1.0)
    for step in range(parts):
        part = part_of(parts, step)
        echo = echoes[step][...] if len(echoes) > 1 else echoes[0][step]
        occupied = echo[2 * bins : 2 * bins + 1].astype(F32)
        model = sum_ref[part].astype(BF16).astype(F32)
        out_ref[part] = (occupied * model - echo[: 2 * bins].astype(F32)).astype(BF16)


def adjoint_body(parts, halo, group, *refs):
    tiles, (even_ref, own_ref, odd_ref, bands_ref) = refs[:3], refs[3:7]
    outs, (blocks_ref, sum_ref) = refs[7 : 7 + parts], refs[7 + parts :]
    even_base, odd_base = side_bases(parts, halo)
    fill_blocks(blocks_ref, [(even_ref, even_base), (own_ref, halo), (odd_ref, odd_base)])
    filter_all(parts, group, tiles, blocks_ref, bands_ref, sum_ref, -1.0)
    for step in range(parts):
        outs[step][...] = sum_ref[part_of(parts, step)].astype(BF16)


def turn_body(parts, matrix_ref, perm_ref, moved_ref, out_ref, sorted_ref):
    def store(side, rows, value):
        sorted_ref[side, rows, :] = value

    columns = half_columns(matrix_ref.shape[1], lax.axis_index("cplx"))
    sorted_matrix(parts, matrix_ref, perm_ref, columns, store)
    for side in range(2):
        out_ref[0, side] = sorted_ref[side].T
        out_ref[1, side] = moved_ref[side].T


def gradient_body(parts, source, step, begun, final, piece_ref, turned_ref, *refs):
    out_ref = refs[-1]
    rows_own = turned_ref.shape[2]
    cells = piece_ref.shape[-1]
    bins = rows_own // parts
    pieces = [piece_ref[...]] if len(piece_ref.shape) == 2 else [piece_ref[n] for n in range(parts)]
    both = jnp.concatenate(
        [jnp.concatenate([x[:bins], x[bins:]], axis=1) for x in pieces], axis=0
    )
    if len(pieces) > 1:
        columns = slice(None)
    else:
        columns = pl.ds(pl.multiple_of(part_of(parts, step) * bins, bins), bins)
    real, imag = [mm(turned_ref[source, side, :, columns], both) for side in range(2)]
    total = [real[:, :cells] + imag[:, cells:], real[:, cells:] - imag[:, :cells]]
    if begun:
        total = [total[0] + refs[0][:, :cells], total[1] + refs[0][:, cells:]]
    if final:
        out_ref[pl.ds(0, rows_own, stride=2), :] = total[0]
        out_ref[pl.ds(1, rows_own, stride=2), :] = total[1]
    else:
        out_ref[:, :cells] = total[0]
        out_ref[:, cells:] = total[1]


def swap_pairs(count, first):
    pairs = []
    for low in range(first, count - 1, 2):
        pairs += [(low, low + 1), (low + 1, low)]
    return pairs


def on_device(image, echoes, slot_time, range_matrix, filter_bank, filter_index):
    rows_own, _, cells = image.shape
    parts, rows_az = lax.axis_size("rg"), lax.axis_size("az")
    bins = rows_own // parts
    bank, _, taps = filter_bank.shape
    halo = taps // 2 // cells
    span = taps // cells + 1
    flip = [(0, 1), (1, 0)]
    struct = jax.ShapeDtypeStruct
    even_pairs, odd_pairs = swap_pairs(rows_az, 0), swap_pairs(rows_az, 1)

    def halves(x):
        return lax.ppermute(x, "cplx", flip)

    def share(pieces):
        if parts == 2:
            return [pieces[0], lax.ppermute(pieces[1], "rg", flip)]
        return [lax.all_to_all(jnp.stack(pieces), "rg", split_axis=0, concat_axis=0)]

    def sides(x):
        if x.ndim == 3 and x.shape[0] > halo:
            first, last = x[:halo], x[x.shape[0] - halo :]
            is_even = lax.rem(lax.axis_index("az"), 2) == 0
            to_even, to_odd = jnp.where(is_even, last, first), jnp.where(is_even, first, last)
        else:
            to_even = to_odd = x
        even = lax.ppermute(to_even, "az", even_pairs)
        odd = lax.ppermute(to_odd, "az", odd_pairs)
        return even, odd

    image_own = image.reshape(2 * rows_own, cells)
    image_other = halves(image_own)
    piece = struct((2 * bins, cells), BF16)
    in_hbm = pl.BlockSpec(memory_space=pltpu.HBM)

    def stay(*arrays):
        return [pltpu.with_memory_space_constraint(x, pltpu.HBM) for x in arrays]

    index_row = filter_index.reshape(1, filter_index.shape[0])
    split_space = pltpu.VMEM((2 * rows_own, cells), F32)
    perms, matrix, begun = call(
        functools.partial(prep_body, parts),
        (
            struct((parts, bins, rows_own), BF16),
            struct(range_matrix.shape, BF16),
            struct((rows_own, 2 * cells), F32),
        ),
        [in_hbm] * 3,
        [
            pltpu.VMEM(index_row.shape, jnp.int32),
            pltpu.VMEM((2 * rows_own, cells), BF16),
            split_space,
            pltpu.SemaphoreType.DMA((3,)),
        ],
        flops=8 * rows_own * rows_own * cells,
    )(*stay(index_row, image_own, range_matrix))
    compressed = [None] * parts
    last = parts - 1
    compressed[last], made = call(
        functools.partial(compress_body, last),
        (piece, struct((rows_own, 2 * cells), BF16)),
        [VMEM] * 4,
        [split_space],
        flops=8 * rows_own * rows_own * cells,
    )(image_other, matrix, perms, begun)
    for step in range(last):
        compressed[step] = call(
            functools.partial(sort_body, step), piece, [VMEM] * 2, flops=4 * rows_own * bins * cells
        )(made, perms)
    own = share(compressed)
    echo_pieces = call(
        functools.partial(echo_body, parts, cells),
        [struct((2 * bins + 16, cells), BF16)] * parts,
        [in_hbm] * 2 + [VMEM],
        [
            pltpu.VMEM((1, slot_time.shape[0]), jnp.int32),
            pltpu.VMEM((2 * rows_own, echoes.shape[2]), BF16),
            split_space,
            pltpu.SemaphoreType.DMA((2,)),
        ],
        flops=4 * rows_own * rows_own * cells,
    )(
        *stay(
            slot_time.reshape(1, slot_time.shape[0]),
            echoes.reshape(2 * rows_own, echoes.shape[2]),
        ),
        perms,
    )
    echo_own = share(echo_pieces)
    pieces, names = [], []
    for step, x in enumerate(own):
        even, odd = sides(x)
        pieces += [x, even, odd]
        names += [("own", step), ("even", step), ("odd", step)]
    group = min(GROUP, bins)
    tile_count = bins // group + 2 * bank + UNROLL
    table_space = pltpu.VMEM((2 * bank, span * cells), F32)
    bands_struct = struct((bank, span * cells, 2 * cells), BF16)
    *tiles, forward_bands = call(
        functools.partial(bands_body, cells, group),
        (
            struct((bank + 2,), jnp.int32),
            struct((tile_count,), jnp.int32),
            struct((tile_count,), jnp.int32),
            bands_struct,
        ),
        [VMEM] * 2,
        [table_space],
        flops=10**9,
        out_specs=(SMEM, SMEM, SMEM, VMEM),
    )(index_row, filter_bank)
    moved = call(
        functools.partial(sort_sent_body, parts),
        struct((2, rows_own, rows_own), BF16),
        [VMEM] * 2,
        flops=4 * rows_own**3,
    )(matrix, perms)
    moved = halves(moved)
    filter_flops = 2 * bins * parts * 2 * span * cells * 2 * cells
    spaces = [
        pltpu.VMEM((parts + 2 * halo, 2 * bins, cells), BF16),
        pltpu.VMEM((parts, 2 * bins, cells), F32),
    ]
    residual = call(
        functools.partial(forward_body, parts, halo, group, names),
        struct((parts, 2 * bins, cells), BF16),
        [SMEM] * 3 + [VMEM] * (len(pieces) + 1 + len(echo_own)),
        spaces,
        flops=filter_flops,
    )(*tiles, *pieces, forward_bands, *echo_own)
    even, odd = sides(residual)
    adjoint_bands = call(
        functools.partial(adjoint_bands_body, cells),
        bands_struct,
        [SMEM, VMEM],
        [table_space],
        flops=10**9,
    )(tiles[0], filter_bank)
    turned = call(
        functools.partial(turn_body, parts),
        struct((2, 2, rows_own, rows_own), BF16),
        [VMEM] * 3,
        [pltpu.VMEM((2, rows_own, rows_own), BF16)],
        flops=4 * rows_own**3,
    )(matrix, perms, moved)
    back = call(
        functools.partial(adjoint_body, parts, halo, group),
        [piece] * parts,
        [SMEM] * 3 + [VMEM] * 4,
        spaces,
        flops=filter_flops,
    )(*tiles, even, residual, odd, adjoint_bands)
    back_own = share(back)
    back_other = []
    for x in back_own:
        back_other.append(halves(x))
    total = None
    for number in range(len(back_own)):
        for source, x in enumerate((back_own[number], back_other[number])):
            final = source == 1 and number == len(back_own) - 1
            args = [x, turned] + ([] if total is None else [total])
            total = call(
                functools.partial(gradient_body, parts, source, number, total is not None, final),
                struct((2 * rows_own, cells) if final else (rows_own, 2 * cells), F32),
                [VMEM] * len(args),
                flops=8 * rows_own * bins * 2 * cells,
            )(*args)
    return total.reshape(rows_own, 2, cells)


def solution(mesh):
    return jax.shard_map(
        on_device,
        mesh=mesh,
        in_specs=(
            P(("frames", "cplx"), None, ("az", "rg")),
            P(("frames", "cplx"), None, ("az", "rg")),
            P(("frames", "az", "rg")),
            P(None, "cplx", None),
            P(),
            P(),
        ),
        out_specs=P(("frames", "cplx"), None, ("az", "rg")),
        check_vma=False,
    )
```

time: 43.3 us -> 44.5 us (1.028)
  Pallas kernels: 13.7 us -> 17 us
  waiting for transfers between devices: 8.26 us -> 5.4 us
  starting transfers between devices: 21 us -> 21.5 us
    pallas_call x9 -> x14, Pallas kernels: 13.7 us -> 17 us  [the longest x1 2.8 us: on_device(): call(functools.partial(bands_body, cells, group), (struct((bank + 2,), jn...]
    ppermute x3, waiting for transfers between devices: 4.74 us -> 2.43 us  [sides(): even = lax.ppermute(to_even, 'az', even_pairs)]
    ppermute x3, starting transfers between devices: 5 us -> 6.31 us  [share(): return [pieces[0], lax.ppermute(pieces[1], 'rg', flip)]]
    ppermute x3, starting transfers between devices: 13.4 us -> 12.5 us  [sides(): even = lax.ppermute(to_even, 'az', even_pairs)]
  transfers between devices with their start and end apart: 13 -> 13, of which waited for: 5 -> 3; matrix products, arithmetic and copies ran while one was open for 0% -> 0% of each run, Pallas kernels for 29% -> 29%
where the time goes in v1:
time: 44.5 us; the launch traced here: 44.1 us
  starting transfers between devices  21.5 us (48%)
  Pallas kernels  17 us (38%)
  waiting for transfers between devices  5.4 us (12%)
    ppermute x3, starting transfers between devices, sides(): even = lax.ppermute(to_even, 'az', even_pairs)  12.5 us
    ppermute x3, starting transfers between devices, share(): return [pieces[0], lax.ppermute(pieces[1], 'rg', flip)]  6.31 us
    ppermute x3, waiting for transfers between devices, share(): return [pieces[0], lax.ppermute(pieces[1], 'rg', flip)]  2.95 us
    pallas_call x1, Pallas kernels, on_device(): call(functools.partial(bands_body, cells, group), (struct((bank + 2,), jn...  2.8 us
    ppermute x3, waiting for transfers between devices, sides(): even = lax.ppermute(to_even, 'az', even_pairs)  2.43 us
    pallas_call x1, Pallas kernels, on_device(): call(functools.partial(prep_body, parts), (struct((parts, bins, rows_own)...  2.17 us
    ppermute x3, starting transfers between devices, sides(): odd = lax.ppermute(to_odd, 'az', odd_pairs)  2 us
    pallas_call x1, Pallas kernels, on_device(): call(functools.partial(adjoint_bands_body, cells), bands_struct, [SMEM, V...  2 us
  transfers between devices with their start and end apart: 13, of which 3 were waited for; matrix products, arithmetic and copies ran while one was open for 0% of the time, Pallas kernels for 29%

profile of v1, /device:TPU:0, one launch (start us, length us, event | category | flops | bytes accessed | tf_op | source)
XLA Modules:
  0.0 44.1 jit_solution(16719755019172733899)
XLA Ops:
  0.0 2.2 %shard_map.65 = (bf16[2,256,512]{2,1,0:T(8,128)(2,1)S(1)}, bf16[2,512,1024]{2,1,0:T(8,128)(2,1)S(1)}, f32[512,256]{1,0:T(8,128)S(1)}) custom-call(s32[1,1024]{1,0:T(1,128)} %bitcast.5, bf16[1024,128]{1,0:T(8,128)(2,1)} %bitcast.7, bf16[2,512,1024]{2,1,0:T(8,128)(2,1)} %matrix_any.1), custom_call_target="tpu_custom_call" | custom-call | flops 268435456 | bytes 3145728 | tf_op jit(solution)/shard_map/pallas_call | solution.py:411
  2.2 0.0 copy-start.2
  2.2 0.7 %shard_map.72 = bf16[2,512,512]{2,1,0:T(8,128)(2,1)S(1)} custom-call(bf16[2,512,1024]{2,1,0:T(8,128)(2,1)S(1)} %get-tuple-element.21.matrix_ref, bf16[2,256,512]{2,1,0:T(8,128)(2,1)S(1)} %get-tuple-element.22.perm_ref), custom_call_target="tpu_custom_call" | custom-call | flops 536870912 | bytes 1048576 | tf_op jit(solution)/shard_map/pallas_call | solution.py:482
  2.9 0.6 %collective-permute-start.11 = (bf16[2,512,512]{2,1,0:T(8,128)(2,1)S(1)}, bf16[2,512,512]{2,1,0:T(8,128)(2,1)S(1)}, u32[]{:S(2)}, u32[]{:S(2)}) collective-permute-start(bf16[2,512,512]{2,1,0:T(8,128)(2,1)S(1)} %shard_map.72), channel_id=1, source_target_pairs={{0,1},{1,0},{2,3},{3,2},{4,5},{5,4},{6,7},{7,6},{8,9},{9,8},{10,11... | collective-permute-start | bytes 3145736 | tf_op jit(solution)/shard_map/ppermute | solution.py:383
  3.5 0.0 copy-done.2
  3.5 0.1 collective-permute-start
  3.6 1.5 %shard_map.68 = (bf16[528,128]{1,0:T(8,128)(2,1)S(1)}, bf16[528,128]{1,0:T(8,128)(2,1)S(1)}) custom-call(s32[1,128]{1,0:T(1,128)} %bitcast.10, bf16[1024,128]{1,0:T(8,128)(2,1)} %bitcast.9, bf16[2,256,512]{2,1,0:T(8,128)(2,1)S(1)} %get-tuple-element.22.perm_ref), custom_call_target="tpu_custom_call" | custom-call | flops 134217728 | bytes 270336 | tf_op jit(solution)/shard_map/pallas_call | solution.py:441
  5.1 2.9 %collective-permute-start.6 = (bf16[528,128]{1,0:T(8,128)(2,1)S(1)}, bf16[528,128]{1,0:T(8,128)(2,1)S(1)}, u32[]{:S(2)}, u32[]{:S(2)}) collective-permute-start(bf16[528,128]{1,0:T(8,128)(2,1)S(1)} %get-tuple-element.28), channel_id=1, source_target_pairs={{0,2},{2,0},{1,3},{3,1},{4,6},{6,4},{5,7},{7,5},{8,10},{10,8},{9,1... | collective-permute-start | bytes 405512 | tf_op jit(solution)/shard_map/ppermute | solution.py:387
  8.0 0.0 collective-permute-done.image_ref
  8.0 0.0 copy-start
  8.0 0.0 copy-start.1
  8.0 0.7 %shard_map.66 = (bf16[512,128]{1,0:T(8,128)(2,1)S(1)}, bf16[512,256]{1,0:T(8,128)(2,1)S(1)}) custom-call(bf16[1024,128]{1,0:T(8,128)(2,1)S(1)} %collective-permute-done.image_ref, bf16[2,512,1024]{2,1,0:T(8,128)(2,1)S(1)} %get-tuple-element.21.matrix_ref, bf16[2,256,512]{2,1,0:T(8,128)(2,1)S(1)} %get-tuple-element.22.perm_ref, ...), custom_call_target="tpu_custom_call" | custom-call | flops 268435456 | bytes 393216 | tf_op jit(solution)/shard_map/pallas_call | solution.py:429
  8.7 1.0 %collective-permute-start.3 = (bf16[512,128]{1,0:T(8,128)(2,1)S(1)}, bf16[512,128]{1,0:T(8,128)(2,1)S(1)}, u32[]{:S(2)}, u32[]{:S(2)}) collective-permute-start(bf16[512,128]{1,0:T(8,128)(2,1)S(1)} %get-tuple-element.25), channel_id=1, source_target_pairs={{0,2},{2,0},{1,3},{3,1},{4,6},{6,4},{5,7},{7,5},{8,10},{10,8},{9,1... | collective-permute-start | bytes 393224 | tf_op jit(solution)/shard_map/ppermute | solution.py:387
  9.8 0.2 shard_map.67.refs_3_
  10.0 0.7 %collective-permute-start.2 = (bf16[512,128]{1,0:T(8,128)(2,1)S(1)}, bf16[512,128]{1,0:T(8,128)(2,1)S(1)}, u32[]{:S(2)}, u32[]{:S(2)}) collective-permute-start(bf16[512,128]{1,0:T(8,128)(2,1)S(1)} %shard_map.67.refs_3_), channel_id=1, source_target_pairs={{4,8},{8,4},{5,9},{9,5},{6,10},{10,6},{7,11},{11,7},{20,24},{24,20... | collective-permute-start | bytes 393224 | tf_op jit(solution)/shard_map/ppermute | solution.py:398
  10.7 4.5 %collective-permute-start.1 = (bf16[512,128]{1,0:T(8,128)(2,1)S(1)}, bf16[512,128]{1,0:T(8,128)(2,1)S(1)}, u32[]{:S(2)}, u32[]{:S(2)}) collective-permute-start(bf16[512,128]{1,0:T(8,128)(2,1)S(1)} %shard_map.67.refs_3_), channel_id=1, source_target_pairs={{0,4},{4,0},{8,12},{12,8},{1,5},{5,1},{9,13},{13,9},{2,6},{6,2},{1... | collective-permute-start | bytes 393224 | tf_op jit(solution)/shard_map/ppermute | solution.py:397
  15.1 0.0 collective-permute-done.3.refs_6_
  15.1 0.7 %collective-permute-start.5 = (bf16[512,128]{1,0:T(8,128)(2,1)S(1)}, bf16[512,128]{1,0:T(8,128)(2,1)S(1)}, u32[]{:S(2)}, u32[]{:S(2)}) collective-permute-start(bf16[512,128]{1,0:T(8,128)(2,1)S(1)} %collective-permute-done.3.refs_6_), channel_id=1, source_target_pairs={{4,8},{8,4},{5,9},{9,5},{6,10},{10,6},{7,11},{11,7},{20,24},{24,20... | collective-permute-start | bytes 393224 | tf_op jit(solution)/shard_map/ppermute | solution.py:398
  15.8 0.0 collective-permute-done.6.refs_11_
  15.8 4.3 %collective-permute-start.4 = (bf16[512,128]{1,0:T(8,128)(2,1)S(1)}, bf16[512,128]{1,0:T(8,128)(2,1)S(1)}, u32[]{:S(2)}, u32[]{:S(2)}) collective-permute-start(bf16[512,128]{1,0:T(8,128)(2,1)S(1)} %collective-permute-done.3.refs_6_), channel_id=1, source_target_pairs={{0,4},{4,0},{8,12},{12,8},{1,5},{5,1},{9,13},{13,9},{2,6},{6,2},{1... | collective-permute-start | bytes 393224 | tf_op jit(solution)/shard_map/ppermute | solution.py:397
  20.1 0.0 copy-done
  20.1 0.0 copy-done.1
  20.1 2.8 %shard_map.64 = (s32[18]{0:T(128)S(1)}, s32[40]{0:T(128)S(1)}, s32[40]{0:T(128)S(1)}, bf16[16,640,256]{2,1,0:T(8,128)(2,1)S(1)}) custom-call(s32[1,1024]{1,0:T(1,128)S(1)} %bitcast.6, bf16[16,2,512]{2,1,0:T(2,128)(2,1)S(1)} %copy-done), custom_call_target="tpu_custom_call" | custom-call | flops 1000000000 | bytes 5243272 | tf_op jit(solution)/shard_map/pallas_call | solution.py:469
  22.9 0.0 collective-permute-done.2.refs_5_
  22.9 0.0 collective-permute-done.1.refs_4_
  22.9 0.0 collective-permute-done.5.refs_8_
  23.0 0.1 collective-permute-done.4.refs_7_
  23.1 1.9 %shard_map.69.refs_4_ = bf16[2,512,128]{2,1,0:T(8,128)(2,1)S(1)} custom-call(s32[18]{0:T(128)S(1)} %get-tuple-element.18.refs_0_.starts_ref, s32[40]{0:T(128)S(1)} %get-tuple-element.19.refs_1_, s32[40]{0:T(128)S(1)} %get-tuple-element.20.refs_2_, bf16[512,128]{1,0:T(8,128)(2,1)S(1)} %shard_map.67.refs_3_, ...), custom_call_target="tpu_custom_call" | custom-call | flops 335544320 | bytes 262144 | tf_op jit(solution)/shard_map/pallas_call | solution.py:494
  25.0 0.7 %collective-permute-start.8 = (bf16[2,512,128]{2,1,0:T(8,128)(2,1)S(1)}, bf16[2,512,128]{2,1,0:T(8,128)(2,1)S(1)}, u32[]{:S(2)}, u32[]{:S(2)}) collective-permute-start(bf16[2,512,128]{2,1,0:T(8,128)(2,1)S(1)} %shard_map.69.refs_4_), channel_id=1, source_target_pairs={{4,8},{8,4},{5,9},{9,5},{6,10},{10,6},{7,11},{11,7},{20,24},{24,20... | collective-permute-start | bytes 786440 | tf_op jit(solution)/shard_map/ppermute | solution.py:398
  25.7 3.8 %collective-permute-start.7 = (bf16[2,512,128]{2,1,0:T(8,128)(2,1)S(1)}, bf16[2,512,128]{2,1,0:T(8,128)(2,1)S(1)}, u32[]{:S(2)}, u32[]{:S(2)}) collective-permute-start(bf16[2,512,128]{2,1,0:T(8,128)(2,1)S(1)} %shard_map.69.refs_4_), channel_id=1, source_target_pairs={{0,4},{4,0},{8,12},{12,8},{1,5},{5,1},{9,13},{13,9},{2,6},{6,2},{1... | collective-permute-start | bytes 786440 | tf_op jit(solution)/shard_map/ppermute | solution.py:397
  29.4 2.0 %shard_map.70.refs_6_ = bf16[16,640,256]{2,1,0:T(8,128)(2,1)S(1)} custom-call(s32[18]{0:T(128)S(1)} %get-tuple-element.18.refs_0_.starts_ref, bf16[16,2,512]{2,1,0:T(2,128)(2,1)S(1)} %copy-done), custom_call_target="tpu_custom_call" | custom-call | flops 1000000000 | bytes 5242880 | tf_op jit(solution)/shard_map/pallas_call | solution.py:502
  31.5 0.0 collective-permute-done.8.refs_5_
  31.5 2.3 %collective-permute-done.7.refs_3_ = bf16[2,512,128]{2,1,0:T(8,128)(2,1)S(1)} collective-permute-done((bf16[2,512,128]{2,1,0:T(8,128)(2,1)S(1)}, bf16[2,512,128]{2,1,0:T(8,128)(2,1)S(1)}, u32[]{:S(2)}, u32[]{:S(2)}) %collective-permute-start.7) | collective-permute-done | bytes 262176 | tf_op jit(solution)/shard_map/ppermute | solution.py:397
  33.8 1.9 %shard_map.71 = (bf16[512,128]{1,0:T(8,128)(2,1)S(1)}, bf16[512,128]{1,0:T(8,128)(2,1)S(1)}) custom-call(s32[18]{0:T(128)S(1)} %get-tuple-element.18.refs_0_.starts_ref, s32[40]{0:T(128)S(1)} %get-tuple-element.19.refs_1_, s32[40]{0:T(128)S(1)} %get-tuple-element.20.refs_2_, bf16[2,512,128]{2,1,0:T(8,128)(2,1)S(1)} %collective-permute-done.7.refs_3_, ...), custom_call_target="tpu_custom_call" | custom-call | flops 335544320 | bytes 262144 | tf_op jit(solution)/shard_map/pallas_call | solution.py:516
  35.7 2.4 %collective-permute-start.9 = (bf16[512,128]{1,0:T(8,128)(2,1)S(1)}, bf16[512,128]{1,0:T(8,128)(2,1)S(1)}, u32[]{:S(2)}, u32[]{:S(2)}) collective-permute-start(bf16[512,128]{1,0:T(8,128)(2,1)S(1)} %get-tuple-element.29), channel_id=1, source_target_pairs={{0,2},{2,0},{1,3},{3,1},{4,6},{6,4},{5,7},{7,5},{8,10},{10,8},{9,1... | collective-permute-start | bytes 393224 | tf_op jit(solution)/shard_map/ppermute | solution.py:387
  38.1 0.0 collective-permute-start.12
  38.1 2.9 %collective-permute-done.9.piece_ref = bf16[512,128]{1,0:T(8,128)(2,1)S(1)} collective-permute-done((bf16[512,128]{1,0:T(8,128)(2,1)S(1)}, bf16[512,128]{1,0:T(8,128)(2,1)S(1)}, u32[]{:S(2)}, u32[]{:S(2)}) %collective-permute-start.9) | collective-permute-done | bytes 131104 | tf_op jit(solution)/shard_map/ppermute | solution.py:387
  41.0 0.0 collective-permute-start.10
  41.0 0.0 collective-permute-done.11.moved_ref
  41.0 1.1 %shard_map.73.turned_ref = bf16[2,2,512,512]{3,2,1,0:T(8,128)(2,1)S(1)} custom-call(bf16[2,512,1024]{2,1,0:T(8,128)(2,1)S(1)} %get-tuple-element.21.matrix_ref, bf16[2,256,512]{2,1,0:T(8,128)(2,1)S(1)} %get-tuple-element.22.perm_ref, bf16[2,512,512]{2,1,0:T(8,128)(2,1)S(1)} %collective-permute-done.11.moved_ref), custom_call_target="tpu_custom_call" | custom-call | flops 536870912 | bytes 2097152 | tf_op jit(solution)/shard_map/pallas_call | solution.py:509
  42.1 0.3 shard_map.74.refs_0_
  42.4 0.0 collective-permute-done.12.piece_ref
  42.4 0.3 shard_map.75.refs_0_
  42.7 0.3 shard_map.76.refs_0_
  43.0 0.0 collective-permute-done.10.piece_ref
  43.0 1.1 %shard_map.77 = f32[1024,128]{1,0:T(8,128)} custom-call(bf16[512,128]{1,0:T(8,128)(2,1)S(1)} %collective-permute-done.10.piece_ref, bf16[2,2,512,512]{3,2,1,0:T(8,128)(2,1)S(1)} %shard_map.73.turned_ref, f32[512,256]{1,0:T(8,128)S(1)} %shard_map.76.refs_0_), custom_call_target="tpu_custom_call" | custom-call | flops 268435456 | bytes 524288 | tf_op jit(solution)/shard_map/pallas_call | solution.py:532
Async XLA Ops:
  2.2 1.3 %copy-start.2 = (bf16[512,2,128]{2,1,0:T(2,128)(2,1)S(1)}, bf16[512,2,128]{2,1,0:T(2,128)(2,1)}, u32[]{:S(2)}) copy-start(bf16[512,2,128]{2,1,0:T(2,128)(2,1)} %param.6) | copy-start | bytes 786436
  2.9 38.1 %collective-permute-start.11 = (bf16[2,512,512]{2,1,0:T(8,128)(2,1)S(1)}, bf16[2,512,512]{2,1,0:T(8,128)(2,1)S(1)}, u32[]{:S(2)}, u32[]{:S(2)}) collective-permute-start(bf16[2,512,512]{2,1,0:T(8,128)(2,1)S(1)} %shard_map.72), channel_id=1, source_target_pairs={{0,1},{1,0},{2,3},{3,2},{4,5},{5,4},{6,7},{7,6},{8,9},{9,8},{10,11... | collective-permute-start | bytes 3145736 | tf_op jit(solution)/shard_map/ppermute | solution.py:383
  3.5 4.5 %collective-permute-start = (bf16[1024,128]{1,0:T(8,128)(2,1)S(1)}, bf16[1024,128]{1,0:T(8,128)(2,1)S(1)}, u32[]{:S(2)}, u32[]{:S(2)}) collective-permute-start(bf16[1024,128]{1,0:T(8,128)(2,1)S(1)} %bitcast.8), channel_id=1, source_target_pairs={{0,1},{1,0},{2,3},{3,2},{4,5},{5,4},{6,7},{7,6},{8,9},{9,8},{10,11... | collective-permute-start | bytes 786440 | tf_op jit(solution)/shard_map/ppermute | solution.py:383
  5.1 10.7 %collective-permute-start.6 = (bf16[528,128]{1,0:T(8,128)(2,1)S(1)}, bf16[528,128]{1,0:T(8,128)(2,1)S(1)}, u32[]{:S(2)}, u32[]{:S(2)}) collective-permute-start(bf16[528,128]{1,0:T(8,128)(2,1)S(1)} %get-tuple-element.28), channel_id=1, source_target_pairs={{0,2},{2,0},{1,3},{3,1},{4,6},{6,4},{5,7},{7,5},{8,10},{10,8},{9,1... | collective-permute-start | bytes 405512 | tf_op jit(solution)/shard_map/ppermute | solution.py:387
  8.0 12.1 %copy-start = (bf16[16,2,512]{2,1,0:T(2,128)(2,1)S(1)}, bf16[16,2,512]{2,1,0:T(2,128)(2,1)}, u32[]{:S(2)}) copy-start(bf16[16,2,512]{2,1,0:T(2,128)(2,1)} %bank_ref.3) | copy-start | bytes 98308
  8.0 12.1 %copy-start.1 = (s32[1024]{0:T(1024)S(1)}, s32[1024]{0:T(1024)}, u32[]{:S(2)}) copy-start(s32[1024]{0:T(1024)} %param.11) | copy-start | bytes 12292
  8.7 6.4 %collective-permute-start.3 = (bf16[512,128]{1,0:T(8,128)(2,1)S(1)}, bf16[512,128]{1,0:T(8,128)(2,1)S(1)}, u32[]{:S(2)}, u32[]{:S(2)}) collective-permute-start(bf16[512,128]{1,0:T(8,128)(2,1)S(1)} %get-tuple-element.25), channel_id=1, source_target_pairs={{0,2},{2,0},{1,3},{3,1},{4,6},{6,4},{5,7},{7,5},{8,10},{10,8},{9,1... | collective-permute-start | bytes 393224 | tf_op jit(solution)/shard_map/ppermute | solution.py:387
  10.0 12.9 %collective-permute-start.2 = (bf16[512,128]{1,0:T(8,128)(2,1)S(1)}, bf16[512,128]{1,0:T(8,128)(2,1)S(1)}, u32[]{:S(2)}, u32[]{:S(2)}) collective-permute-start(bf16[512,128]{1,0:T(8,128)(2,1)S(1)} %shard_map.67.refs_3_), channel_id=1, source_target_pairs={{4,8},{8,4},{5,9},{9,5},{6,10},{10,6},{7,11},{11,7},{20,24},{24,20... | collective-permute-start | bytes 393224 | tf_op jit(solution)/shard_map/ppermute | solution.py:398
  10.7 12.2 %collective-permute-start.1 = (bf16[512,128]{1,0:T(8,128)(2,1)S(1)}, bf16[512,128]{1,0:T(8,128)(2,1)S(1)}, u32[]{:S(2)}, u32[]{:S(2)}) collective-permute-start(bf16[512,128]{1,0:T(8,128)(2,1)S(1)} %shard_map.67.refs_3_), channel_id=1, source_target_pairs={{0,4},{4,0},{8,12},{12,8},{1,5},{5,1},{9,13},{13,9},{2,6},{6,2},{1... | collective-permute-start | bytes 393224 | tf_op jit(solution)/shard_map/ppermute | solution.py:397
  15.1 7.8 %collective-permute-start.5 = (bf16[512,128]{1,0:T(8,128)(2,1)S(1)}, bf16[512,128]{1,0:T(8,128)(2,1)S(1)}, u32[]{:S(2)}, u32[]{:S(2)}) collective-permute-start(bf16[512,128]{1,0:T(8,128)(2,1)S(1)} %collective-permute-done.3.refs_6_), channel_id=1, source_target_pairs={{4,8},{8,4},{5,9},{9,5},{6,10},{10,6},{7,11},{11,7},{20,24},{24,20... | collective-permute-start | bytes 393224 | tf_op jit(solution)/shard_map/ppermute | solution.py:398
  15.8 7.2 %collective-permute-start.4 = (bf16[512,128]{1,0:T(8,128)(2,1)S(1)}, bf16[512,128]{1,0:T(8,128)(2,1)S(1)}, u32[]{:S(2)}, u32[]{:S(2)}) collective-permute-start(bf16[512,128]{1,0:T(8,128)(2,1)S(1)} %collective-permute-done.3.refs_6_), channel_id=1, source_target_pairs={{0,4},{4,0},{8,12},{12,8},{1,5},{5,1},{9,13},{13,9},{2,6},{6,2},{1... | collective-permute-start | bytes 393224 | tf_op jit(solution)/shard_map/ppermute | solution.py:397
  25.0 6.5 %collective-permute-start.8 = (bf16[2,512,128]{2,1,0:T(8,128)(2,1)S(1)}, bf16[2,512,128]{2,1,0:T(8,128)(2,1)S(1)}, u32[]{:S(2)}, u32[]{:S(2)}) collective-permute-start(bf16[2,512,128]{2,1,0:T(8,128)(2,1)S(1)} %shard_map.69.refs_4_), channel_id=1, source_target_pairs={{4,8},{8,4},{5,9},{9,5},{6,10},{10,6},{7,11},{11,7},{20,24},{24,20... | collective-permute-start | bytes 786440 | tf_op jit(solution)/shard_map/ppermute | solution.py:398
  25.7 8.1 %collective-permute-start.7 = (bf16[2,512,128]{2,1,0:T(8,128)(2,1)S(1)}, bf16[2,512,128]{2,1,0:T(8,128)(2,1)S(1)}, u32[]{:S(2)}, u32[]{:S(2)}) collective-permute-start(bf16[2,512,128]{2,1,0:T(8,128)(2,1)S(1)} %shard_map.69.refs_4_), channel_id=1, source_target_pairs={{0,4},{4,0},{8,12},{12,8},{1,5},{5,1},{9,13},{13,9},{2,6},{6,2},{1... | collective-permute-start | bytes 786440 | tf_op jit(solution)/shard_map/ppermute | solution.py:397
  35.7 5.3 %collective-permute-start.9 = (bf16[512,128]{1,0:T(8,128)(2,1)S(1)}, bf16[512,128]{1,0:T(8,128)(2,1)S(1)}, u32[]{:S(2)}, u32[]{:S(2)}) collective-permute-start(bf16[512,128]{1,0:T(8,128)(2,1)S(1)} %get-tuple-element.29), channel_id=1, source_target_pairs={{0,2},{2,0},{1,3},{3,1},{4,6},{6,4},{5,7},{7,5},{8,10},{10,8},{9,1... | collective-permute-start | bytes 393224 | tf_op jit(solution)/shard_map/ppermute | solution.py:387
  38.1 4.3 %collective-permute-start.12 = (bf16[512,128]{1,0:T(8,128)(2,1)S(1)}, bf16[512,128]{1,0:T(8,128)(2,1)S(1)}, u32[]{:S(2)}, u32[]{:S(2)}) collective-permute-start(bf16[512,128]{1,0:T(8,128)(2,1)S(1)} %get-tuple-element.30.piece_ref), channel_id=1, source_target_pairs={{0,1},{1,0},{2,3},{3,2},{4,5},{5,4},{6,7},{7,6},{8,9},{9,8},{10,11... | collective-permute-start | bytes 393224 | tf_op jit(solution)/shard_map/ppermute | solution.py:383
  41.0 2.0 %collective-permute-start.10 = (bf16[512,128]{1,0:T(8,128)(2,1)S(1)}, bf16[512,128]{1,0:T(8,128)(2,1)S(1)}, u32[]{:S(2)}, u32[]{:S(2)}) collective-permute-start(bf16[512,128]{1,0:T(8,128)(2,1)S(1)} %collective-permute-done.9.piece_ref), channel_id=1, source_target_pairs={{0,1},{1,0},{2,3},{3,2},{4,5},{5,4},{6,7},{7,6},{8,9},{9,8},{10,11... | collective-permute-start | bytes 393224 | tf_op jit(solution)/shard_map/ppermute | solution.py:383

commit v2 on v1

--- a/solution.py
+++ b/solution.py
@@ -75,8 +75,34 @@
     return pl.ds(pl.multiple_of(half * rows_own, rows_own), rows_own)
 
 
-def prep_body(parts, index_any, image_any, matrix_any, *rest):
-    perm_ref, matrix_ref, begun_ref, index_ref, image_ref, tmp_ref, sems = rest
+def list_tiles(ids, group, starts_ref, number_ref, first_ref):
+    bank, bins = starts_ref.shape[0] - 2, ids.shape[1] // lax.axis_size("rg")
+    base = lax.axis_index("rg") * bins
+    for number in range(bank + 1):
+        before = jnp.sum((ids < number).astype(F32)).astype(jnp.int32)
+        starts_ref[number] = jnp.clip(before - base, 0, bins)
+
+    def per_filter(number, count):
+        low, high = starts_ref[number], starts_ref[number + 1]
+        aligned = lax.div(low, ALIGN) * ALIGN
+
+        def per_tile(at, count):
+            number_ref[count] = number
+            first_ref[count] = jnp.minimum(aligned + at * group, bins - group)
+            return count + 1
+
+        tiles = jnp.where(high > low, lax.div(high - aligned + (group - 1), group), 0)
+        return lax.fori_loop(0, tiles, per_tile, count)
+
+    count = lax.fori_loop(0, bank, per_filter, 0)
+    starts_ref[bank + 1] = count
+    for extra in range(UNROLL - 1):
+        number_ref[count + extra] = number_ref[count - 1]
+        first_ref[count + extra] = first_ref[count - 1]
+
+
+def prep_body(parts, group, index_any, image_any, matrix_any, *rest):
+    tiles, (perm_ref, matrix_ref, begun_ref, index_ref, image_ref, tmp_ref, sems) = rest[:3], rest[3:]
     bins, rows_own = perm_ref.shape[1:]
     half = lax.axis_index("cplx")
     loads = [
@@ -88,10 +114,12 @@
     for load in loads:
         load.start()
     loads[0].wait()
-    rank = rank_of(index_ref[:, half_columns(rows_own, half)])
+    ids = index_ref[:, half_columns(rows_own, half)]
+    rank = rank_of(ids)
     for step in range(parts):
         slot = (iota((bins, 1), 0) + part_of(parts, step) * bins).astype(F32)
         perm_ref[step] = (slot == rank).astype(BF16)
+    list_tiles(ids, group, *tiles)
     loads[1].wait()
     image = split_complex(tmp_ref, image_ref[...].astype(F32))
     loads[2].wait()
@@ -133,43 +161,12 @@
     make_bands(seg, starts_ref, table_ref, bands_ref)
 
 
-def list_tiles(ids, group, starts_ref, number_ref, first_ref):
-    bank, bins = starts_ref.shape[0] - 2, ids.shape[1] // lax.axis_size("rg")
-    base = lax.axis_index("rg") * bins
-    for number in range(bank + 1):
-        before = jnp.sum((ids < number).astype(F32)).astype(jnp.int32)
-        starts_ref[number] = jnp.clip(before - base, 0, bins)
-
-    def per_filter(number, count):
-        low, high = starts_ref[number], starts_ref[number + 1]
-        aligned = lax.div(low, ALIGN) * ALIGN
-
-        def per_tile(at, count):
-            number_ref[count] = number
-            first_ref[count] = jnp.minimum(aligned + at * group, bins - group)
-            return count + 1
-
-        tiles = jnp.where(high > low, lax.div(high - aligned + (group - 1), group), 0)
-        return lax.fori_loop(0, tiles, per_tile, count)
-
-    count = lax.fori_loop(0, bank, per_filter, 0)
-    starts_ref[bank + 1] = count
-    for extra in range(UNROLL - 1):
-        number_ref[count + extra] = number_ref[count - 1]
-        first_ref[count + extra] = first_ref[count - 1]
-
-
-def bands_body(cell_count, group, index_ref, bank_ref, *rest):
-    starts_ref, number_ref, first_ref, bands_ref, table_ref = rest
-    _, _, taps = bank_ref.shape
-    rows_own = index_ref.shape[1] // lax.axis_size("cplx")
-    ids = index_ref[:, half_columns(rows_own, lax.axis_index("cplx"))]
-    list_tiles(ids, group, starts_ref, number_ref, first_ref)
+def forward_bands_body(seg, starts_ref, bank_ref, bands_ref, table_ref):
     fill_table(bank_ref, table_ref)
-    width = table_ref.shape[1]
+    taps, width = bank_ref.shape[2], table_ref.shape[1]
     turn = (iota((taps, width), 0) + iota((taps, width), 1) == taps).astype(BF16)
     table_ref[...] = mm(table_ref[:, :taps].astype(BF16), turn)
-    make_bands(cell_count, starts_ref, table_ref, bands_ref)
+    make_bands(seg, starts_ref, table_ref, bands_ref)
 
 
 def echo_body(parts, cell_count, time_any, echo_any, perm_ref, *rest):
@@ -408,9 +405,14 @@
 
     index_row = filter_index.reshape(1, filter_index.shape[0])
     split_space = pltpu.VMEM((2 * rows_own, cells), F32)
-    perms, matrix, begun = call(
-        functools.partial(prep_body, parts),
+    group = min(GROUP, bins)
+    tile_list = struct((bins // group + 2 * bank + UNROLL,), jnp.int32)
+    *tiles, perms, matrix, begun = call(
+        functools.partial(prep_body, parts, group),
         (
+            struct((bank + 2,), jnp.int32),
+            tile_list,
+            tile_list,
             struct((parts, bins, rows_own), BF16),
             struct(range_matrix.shape, BF16),
             struct((rows_own, 2 * cells), F32),
@@ -423,6 +425,7 @@
             pltpu.SemaphoreType.DMA((3,)),
         ],
         flops=8 * rows_own * rows_own * cells,
+        out_specs=(SMEM, SMEM, SMEM, VMEM, VMEM, VMEM),
     )(*stay(index_row, image_own, range_matrix))
     compressed = [None] * parts
     last = parts - 1
@@ -462,23 +465,15 @@
         even, odd = sides(x)
         pieces += [x, even, odd]
         names += [("own", step), ("even", step), ("odd", step)]
-    group = min(GROUP, bins)
-    tile_count = bins // group + 2 * bank + UNROLL
     table_space = pltpu.VMEM((2 * bank, span * cells), F32)
     bands_struct = struct((bank, span * cells, 2 * cells), BF16)
-    *tiles, forward_bands = call(
-        functools.partial(bands_body, cells, group),
-        (
-            struct((bank + 2,), jnp.int32),
-            struct((tile_count,), jnp.int32),
-            struct((tile_count,), jnp.int32),
-            bands_struct,
-        ),
-        [VMEM] * 2,
+    forward_bands = call(
+        functools.partial(forward_bands_body, cells),
+        bands_struct,
+        [SMEM, VMEM],
         [table_space],
         flops=10**9,
-        out_specs=(SMEM, SMEM, SMEM, VMEM),
-    )(index_row, filter_bank)
+    )(tiles[0], filter_bank)
     moved = call(
         functools.partial(sort_sent_body, parts),
         struct((2, rows_own, rows_own), BF16),

time: 44.5 us -> 44.1 us (level)
  the two profiles are of different devices: /device:TPU:0 before, /device:TPU:19 now
where the time goes in v2:
time: 44.1 us; the launch traced here: 43.9 us
  starting transfers between devices  19.6 us (44%)
  Pallas kernels  16.8 us (38%)
  waiting for transfers between devices  7.24 us (16%)
    ppermute x4, starting transfers between devices, halves(): return lax.ppermute(x, 'cplx', flip)  9.91 us
    ppermute x3, starting transfers between devices, sides(): odd = lax.ppermute(to_odd, 'az', odd_pairs)  5.78 us
    ppermute x3, waiting for transfers between devices, sides(): odd = lax.ppermute(to_odd, 'az', odd_pairs)  3.62 us
    ppermute x3, starting transfers between devices, sides(): even = lax.ppermute(to_even, 'az', even_pairs)  2.73 us
    pallas_call x1, Pallas kernels, on_device(): call(functools.partial(prep_body, parts, group), (struct((bank + 2,), jnp...  2.34 us
    pallas_call x1, Pallas kernels, on_device(): call(functools.partial(forward_bands_body, cells), bands_struct, [SMEM, V...  2.31 us
    pallas_call x1, Pallas kernels, on_device(): call(functools.partial(adjoint_bands_body, cells), bands_struct, [SMEM, V...  2.16 us
    pallas_call x4, Pallas kernels, on_device(): call(functools.partial(gradient_body, parts, source, number, total is not...  1.97 us
  transfers between devices with their start and end apart: 13, of which 5 were waited for; matrix products, arithmetic and copies ran while one was open for 0% of the time, Pallas kernels for 29%

profile of v2, /device:TPU:19, one launch (start us, length us, event | category | flops | bytes accessed | tf_op | source)
XLA Modules:
  0.0 43.9 jit_solution(12745280103766175869)
XLA Ops:
  0.0 2.3 %shard_map.64 = (s32[18]{0:T(128)S(1)}, s32[40]{0:T(128)S(1)}, s32[40]{0:T(128)S(1)}, bf16[2,256,512]{2,1,0:T(8,128)(2,1)S(1)}, bf16[2,512,1024]{2,1,0:T(8,128)(2,1)S(1)}, /*index=5*/f32[512,256]{1,0:T(8,128)S(1)}) custom-call(s32[1,1024]{1,0:T(1,128)} %bitcast.8, bf16[1024,128]{1,0:T(8,128)(2,1)} %bitcast.5, bf16[2,512,1024]{2,1,0:T(8,128)(2,1)} %matrix_any.1), custom_call_target="tpu_custom_call" | custom-call | flops 268435456 | bytes 3146120 | tf_op jit(solution)/shard_map/pallas_call | solution.py:410
  2.3 0.0 copy-start.1
  2.4 0.7 %shard_map.72 = bf16[2,512,512]{2,1,0:T(8,128)(2,1)S(1)} custom-call(bf16[2,512,1024]{2,1,0:T(8,128)(2,1)S(1)} %get-tuple-element.20.matrix_ref, bf16[2,256,512]{2,1,0:T(8,128)(2,1)S(1)} %get-tuple-element.21.perm_ref), custom_call_target="tpu_custom_call" | custom-call | flops 536870912 | bytes 1048576 | tf_op jit(solution)/shard_map/pallas_call | solution.py:477
  3.1 0.7 %collective-permute-start.11 = (bf16[2,512,512]{2,1,0:T(8,128)(2,1)S(1)}, bf16[2,512,512]{2,1,0:T(8,128)(2,1)S(1)}, u32[]{:S(2)}, u32[]{:S(2)}) collective-permute-start(bf16[2,512,512]{2,1,0:T(8,128)(2,1)S(1)} %shard_map.72), channel_id=1, source_target_pairs={{0,1},{1,0},{2,3},{3,2},{4,5},{5,4},{6,7},{7,6},{8,9},{9,8},{10,11... | collective-permute-start | bytes 3145736 | tf_op jit(solution)/shard_map/ppermute | solution.py:380
  3.8 0.0 copy-done.1
  3.8 0.1 collective-permute-start
  4.0 1.5 %shard_map.68 = (bf16[528,128]{1,0:T(8,128)(2,1)S(1)}, bf16[528,128]{1,0:T(8,128)(2,1)S(1)}) custom-call(s32[1,128]{1,0:T(1,128)} %bitcast.9, bf16[1024,128]{1,0:T(8,128)(2,1)} %bitcast.7, bf16[2,256,512]{2,1,0:T(8,128)(2,1)S(1)} %get-tuple-element.21.perm_ref), custom_call_target="tpu_custom_call" | custom-call | flops 134217728 | bytes 270336 | tf_op jit(solution)/shard_map/pallas_call | solution.py:444
  5.5 0.3 collective-permute-start.6
  5.8 0.7 %collective-permute-done.image_ref = bf16[1024,128]{1,0:T(8,128)(2,1)S(1)} collective-permute-done((bf16[1024,128]{1,0:T(8,128)(2,1)S(1)}, bf16[1024,128]{1,0:T(8,128)(2,1)S(1)}, u32[]{:S(2)}, u32[]{:S(2)}) %collective-permute-start) | collective-permute-done | bytes 262176 | tf_op jit(solution)/shard_map/ppermute | solution.py:380
  6.5 0.0 copy-start
  6.5 0.7 %shard_map.65 = (bf16[512,128]{1,0:T(8,128)(2,1)S(1)}, bf16[512,256]{1,0:T(8,128)(2,1)S(1)}) custom-call(bf16[1024,128]{1,0:T(8,128)(2,1)S(1)} %collective-permute-done.image_ref, bf16[2,512,1024]{2,1,0:T(8,128)(2,1)S(1)} %get-tuple-element.20.matrix_ref, bf16[2,256,512]{2,1,0:T(8,128)(2,1)S(1)} %get-tuple-element.21.perm_ref, ...), custom_call_target="tpu_custom_call" | custom-call | flops 268435456 | bytes 393216 | tf_op jit(solution)/shard_map/pallas_call | solution.py:432
  7.2 0.6 %collective-permute-start.3 = (bf16[512,128]{1,0:T(8,128)(2,1)S(1)}, bf16[512,128]{1,0:T(8,128)(2,1)S(1)}, u32[]{:S(2)}, u32[]{:S(2)}) collective-permute-start(bf16[512,128]{1,0:T(8,128)(2,1)S(1)} %get-tuple-element.24), channel_id=1, source_target_pairs={{0,2},{2,0},{1,3},{3,1},{4,6},{6,4},{5,7},{7,5},{8,10},{10,8},{9,1... | collective-permute-start | bytes 393224 | tf_op jit(solution)/shard_map/ppermute | solution.py:384
  7.8 0.2 shard_map.66.refs_3_
  8.0 1.4 %collective-permute-start.1 = (bf16[512,128]{1,0:T(8,128)(2,1)S(1)}, bf16[512,128]{1,0:T(8,128)(2,1)S(1)}, u32[]{:S(2)}, u32[]{:S(2)}) collective-permute-start(bf16[512,128]{1,0:T(8,128)(2,1)S(1)} %shard_map.66.refs_3_), channel_id=1, source_target_pairs={{0,4},{4,0},{8,12},{12,8},{1,5},{5,1},{9,13},{13,9},{2,6},{6,2},{1... | collective-permute-start | bytes 393224 | tf_op jit(solution)/shard_map/ppermute | solution.py:394
  9.4 1.9 %collective-permute-start.2 = (bf16[512,128]{1,0:T(8,128)(2,1)S(1)}, bf16[512,128]{1,0:T(8,128)(2,1)S(1)}, u32[]{:S(2)}, u32[]{:S(2)}) collective-permute-start(bf16[512,128]{1,0:T(8,128)(2,1)S(1)} %shard_map.66.refs_3_), channel_id=1, source_target_pairs={{4,8},{8,4},{5,9},{9,5},{6,10},{10,6},{7,11},{11,7},{20,24},{24,20... | collective-permute-start | bytes 393224 | tf_op jit(solution)/shard_map/ppermute | solution.py:395
  11.3 1.8 %collective-permute-done.3.refs_6_ = bf16[512,128]{1,0:T(8,128)(2,1)S(1)} collective-permute-done((bf16[512,128]{1,0:T(8,128)(2,1)S(1)}, bf16[512,128]{1,0:T(8,128)(2,1)S(1)}, u32[]{:S(2)}, u32[]{:S(2)}) %collective-permute-start.3) | collective-permute-done | bytes 131104 | tf_op jit(solution)/shard_map/ppermute | solution.py:384
  13.1 1.3 %collective-permute-start.4 = (bf16[512,128]{1,0:T(8,128)(2,1)S(1)}, bf16[512,128]{1,0:T(8,128)(2,1)S(1)}, u32[]{:S(2)}, u32[]{:S(2)}) collective-permute-start(bf16[512,128]{1,0:T(8,128)(2,1)S(1)} %collective-permute-done.3.refs_6_), channel_id=1, source_target_pairs={{0,4},{4,0},{8,12},{12,8},{1,5},{5,1},{9,13},{13,9},{2,6},{6,2},{1... | collective-permute-start | bytes 393224 | tf_op jit(solution)/shard_map/ppermute | solution.py:394
  14.4 0.0 collective-permute-done.6.refs_11_
  14.4 1.9 %collective-permute-start.5 = (bf16[512,128]{1,0:T(8,128)(2,1)S(1)}, bf16[512,128]{1,0:T(8,128)(2,1)S(1)}, u32[]{:S(2)}, u32[]{:S(2)}) collective-permute-start(bf16[512,128]{1,0:T(8,128)(2,1)S(1)} %collective-permute-done.3.refs_6_), channel_id=1, source_target_pairs={{4,8},{8,4},{5,9},{9,5},{6,10},{10,6},{7,11},{11,7},{20,24},{24,20... | collective-permute-start | bytes 393224 | tf_op jit(solution)/shard_map/ppermute | solution.py:395
  16.3 0.0 copy-done
  16.3 2.3 %shard_map.67.refs_9_ = bf16[16,640,256]{2,1,0:T(8,128)(2,1)S(1)} custom-call(s32[18]{0:T(128)S(1)} %get-tuple-element.17.starts_ref.refs_0_, bf16[16,2,512]{2,1,0:T(2,128)(2,1)S(1)} %copy-done), custom_call_target="tpu_custom_call" | custom-call | flops 1000000000 | bytes 5242880 | tf_op jit(solution)/shard_map/pallas_call | solution.py:470
  18.7 0.0 collective-permute-done.1.refs_4_
  18.7 0.0 collective-permute-done.2.refs_5_
  18.7 0.0 collective-permute-done.4.refs_7_
  18.7 1.4 %collective-permute-done.5.refs_8_ = bf16[512,128]{1,0:T(8,128)(2,1)S(1)} collective-permute-done((bf16[512,128]{1,0:T(8,128)(2,1)S(1)}, bf16[512,128]{1,0:T(8,128)(2,1)S(1)}, u32[]{:S(2)}, u32[]{:S(2)}) %collective-permute-start.5) | collective-permute-done | bytes 131104 | tf_op jit(solution)/shard_map/ppermute | solution.py:395
  20.1 1.9 %shard_map.69.refs_4_ = bf16[2,512,128]{2,1,0:T(8,128)(2,1)S(1)} custom-call(s32[18]{0:T(128)S(1)} %get-tuple-element.17.starts_ref.refs_0_, s32[40]{0:T(128)S(1)} %get-tuple-element.18.refs_1_, s32[40]{0:T(128)S(1)} %get-tuple-element.19.refs_2_, bf16[512,128]{1,0:T(8,128)(2,1)S(1)} %shard_map.66.refs_3_, ...), custom_call_target="tpu_custom_call" | custom-call | flops 335544320 | bytes 262144 | tf_op jit(solution)/shard_map/pallas_call | solution.py:489
  22.1 0.1 collective-permute-start.7
  22.2 2.0 %collective-permute-start.8 = (bf16[2,512,128]{2,1,0:T(8,128)(2,1)S(1)}, bf16[2,512,128]{2,1,0:T(8,128)(2,1)S(1)}, u32[]{:S(2)}, u32[]{:S(2)}) collective-permute-start(bf16[2,512,128]{2,1,0:T(8,128)(2,1)S(1)} %shard_map.69.refs_4_), channel_id=1, source_target_pairs={{4,8},{8,4},{5,9},{9,5},{6,10},{10,6},{7,11},{11,7},{20,24},{24,20... | collective-permute-start | bytes 786440 | tf_op jit(solution)/shard_map/ppermute | solution.py:395
  24.1 2.2 %shard_map.70.refs_6_ = bf16[16,640,256]{2,1,0:T(8,128)(2,1)S(1)} custom-call(s32[18]{0:T(128)S(1)} %get-tuple-element.17.starts_ref.refs_0_, bf16[16,2,512]{2,1,0:T(2,128)(2,1)S(1)} %copy-done), custom_call_target="tpu_custom_call" | custom-call | flops 1000000000 | bytes 5242880 | tf_op jit(solution)/shard_map/pallas_call | solution.py:497
  26.3 1.1 %collective-permute-done.7.refs_3_ = bf16[2,512,128]{2,1,0:T(8,128)(2,1)S(1)} collective-permute-done((bf16[2,512,128]{2,1,0:T(8,128)(2,1)S(1)}, bf16[2,512,128]{2,1,0:T(8,128)(2,1)S(1)}, u32[]{:S(2)}, u32[]{:S(2)}) %collective-permute-start.7) | collective-permute-done | bytes 262176 | tf_op jit(solution)/shard_map/ppermute | solution.py:394
  27.4 2.2 %collective-permute-done.8.refs_5_ = bf16[2,512,128]{2,1,0:T(8,128)(2,1)S(1)} collective-permute-done((bf16[2,512,128]{2,1,0:T(8,128)(2,1)S(1)}, bf16[2,512,128]{2,1,0:T(8,128)(2,1)S(1)}, u32[]{:S(2)}, u32[]{:S(2)}) %collective-permute-start.8) | collective-permute-done | bytes 262176 | tf_op jit(solution)/shard_map/ppermute | solution.py:395
  29.6 1.9 %shard_map.71 = (bf16[512,128]{1,0:T(8,128)(2,1)S(1)}, bf16[512,128]{1,0:T(8,128)(2,1)S(1)}) custom-call(s32[18]{0:T(128)S(1)} %get-tuple-element.17.starts_ref.refs_0_, s32[40]{0:T(128)S(1)} %get-tuple-element.18.refs_1_, s32[40]{0:T(128)S(1)} %get-tuple-element.19.refs_2_, bf16[2,512,128]{2,1,0:T(8,128)(2,1)S(1)} %collective-permute-done.7.refs_3_, ...), custom_call_target="tpu_custom_call" | custom-call | flops 335544320 | bytes 262144 | tf_op jit(solution)/shard_map/pallas_call | solution.py:511
  31.5 0.3 collective-permute-start.9
  31.8 4.1 %collective-permute-start.12 = (bf16[512,128]{1,0:T(8,128)(2,1)S(1)}, bf16[512,128]{1,0:T(8,128)(2,1)S(1)}, u32[]{:S(2)}, u32[]{:S(2)}) collective-permute-start(bf16[512,128]{1,0:T(8,128)(2,1)S(1)} %get-tuple-element.28.piece_ref), channel_id=1, source_target_pairs={{0,1},{1,0},{2,3},{3,2},{4,5},{5,4},{6,7},{7,6},{8,9},{9,8},{10,11... | collective-permute-start | bytes 393224 | tf_op jit(solution)/shard_map/ppermute | solution.py:380
  35.9 0.0 collective-permute-done.9.piece_ref
  35.9 4.9 %collective-permute-start.10 = (bf16[512,128]{1,0:T(8,128)(2,1)S(1)}, bf16[512,128]{1,0:T(8,128)(2,1)S(1)}, u32[]{:S(2)}, u32[]{:S(2)}) collective-permute-start(bf16[512,128]{1,0:T(8,128)(2,1)S(1)} %collective-permute-done.9.piece_ref), channel_id=1, source_target_pairs={{0,1},{1,0},{2,3},{3,2},{4,5},{5,4},{6,7},{7,6},{8,9},{9,8},{10,11... | collective-permute-start | bytes 393224 | tf_op jit(solution)/shard_map/ppermute | solution.py:380
  40.8 0.0 collective-permute-done.11.moved_ref
  40.8 1.1 %shard_map.73.turned_ref = bf16[2,2,512,512]{3,2,1,0:T(8,128)(2,1)S(1)} custom-call(bf16[2,512,1024]{2,1,0:T(8,128)(2,1)S(1)} %get-tuple-element.20.matrix_ref, bf16[2,256,512]{2,1,0:T(8,128)(2,1)S(1)} %get-tuple-element.21.perm_ref, bf16[2,512,512]{2,1,0:T(8,128)(2,1)S(1)} %collective-permute-done.11.moved_ref), custom_call_target="tpu_custom_call" | custom-call | flops 536870912 | bytes 2097152 | tf_op jit(solution)/shard_map/pallas_call | solution.py:504
  41.9 0.3 shard_map.74.refs_0_
  42.2 0.0 collective-permute-done.12.piece_ref
  42.2 0.3 shard_map.75.refs_0_
  42.5 0.3 shard_map.76.refs_0_
  42.8 0.0 collective-permute-done.10.piece_ref
  42.8 1.1 %shard_map.77 = f32[1024,128]{1,0:T(8,128)} custom-call(bf16[512,128]{1,0:T(8,128)(2,1)S(1)} %collective-permute-done.10.piece_ref, bf16[2,2,512,512]{3,2,1,0:T(8,128)(2,1)S(1)} %shard_map.73.turned_ref, f32[512,256]{1,0:T(8,128)S(1)} %shard_map.76.refs_0_), custom_call_target="tpu_custom_call" | custom-call | flops 268435456 | bytes 524288 | tf_op jit(solution)/shard_map/pallas_call | solution.py:527
Async XLA Ops:
  2.3 1.5 %copy-start.1 = (bf16[512,2,128]{2,1,0:T(2,128)(2,1)S(1)}, bf16[512,2,128]{2,1,0:T(2,128)(2,1)}, u32[]{:S(2)}) copy-start(bf16[512,2,128]{2,1,0:T(2,128)(2,1)} %param.6) | copy-start | bytes 786436
  3.1 37.7 %collective-permute-start.11 = (bf16[2,512,512]{2,1,0:T(8,128)(2,1)S(1)}, bf16[2,512,512]{2,1,0:T(8,128)(2,1)S(1)}, u32[]{:S(2)}, u32[]{:S(2)}) collective-permute-start(bf16[2,512,512]{2,1,0:T(8,128)(2,1)S(1)} %shard_map.72), channel_id=1, source_target_pairs={{0,1},{1,0},{2,3},{3,2},{4,5},{5,4},{6,7},{7,6},{8,9},{9,8},{10,11... | collective-permute-start | bytes 3145736 | tf_op jit(solution)/shard_map/ppermute | solution.py:380
  3.8 2.7 %collective-permute-start = (bf16[1024,128]{1,0:T(8,128)(2,1)S(1)}, bf16[1024,128]{1,0:T(8,128)(2,1)S(1)}, u32[]{:S(2)}, u32[]{:S(2)}) collective-permute-start(bf16[1024,128]{1,0:T(8,128)(2,1)S(1)} %bitcast.6), channel_id=1, source_target_pairs={{0,1},{1,0},{2,3},{3,2},{4,5},{5,4},{6,7},{7,6},{8,9},{9,8},{10,11... | collective-permute-start | bytes 786440 | tf_op jit(solution)/shard_map/ppermute | solution.py:380
  5.5 9.0 %collective-permute-start.6 = (bf16[528,128]{1,0:T(8,128)(2,1)S(1)}, bf16[528,128]{1,0:T(8,128)(2,1)S(1)}, u32[]{:S(2)}, u32[]{:S(2)}) collective-permute-start(bf16[528,128]{1,0:T(8,128)(2,1)S(1)} %get-tuple-element.26), channel_id=1, source_target_pairs={{0,2},{2,0},{1,3},{3,1},{4,6},{6,4},{5,7},{7,5},{8,10},{10,8},{9,1... | collective-permute-start | bytes 405512 | tf_op jit(solution)/shard_map/ppermute | solution.py:384
  6.5 9.9 %copy-start = (bf16[16,2,512]{2,1,0:T(2,128)(2,1)S(1)}, bf16[16,2,512]{2,1,0:T(2,128)(2,1)}, u32[]{:S(2)}) copy-start(bf16[16,2,512]{2,1,0:T(2,128)(2,1)} %bank_ref.3) | copy-start | bytes 98308
  7.2 5.9 %collective-permute-start.3 = (bf16[512,128]{1,0:T(8,128)(2,1)S(1)}, bf16[512,128]{1,0:T(8,128)(2,1)S(1)}, u32[]{:S(2)}, u32[]{:S(2)}) collective-permute-start(bf16[512,128]{1,0:T(8,128)(2,1)S(1)} %get-tuple-element.24), channel_id=1, source_target_pairs={{0,2},{2,0},{1,3},{3,1},{4,6},{6,4},{5,7},{7,5},{8,10},{10,8},{9,1... | collective-permute-start | bytes 393224 | tf_op jit(solution)/shard_map/ppermute | solution.py:384
  8.0 10.7 %collective-permute-start.1 = (bf16[512,128]{1,0:T(8,128)(2,1)S(1)}, bf16[512,128]{1,0:T(8,128)(2,1)S(1)}, u32[]{:S(2)}, u32[]{:S(2)}) collective-permute-start(bf16[512,128]{1,0:T(8,128)(2,1)S(1)} %shard_map.66.refs_3_), channel_id=1, source_target_pairs={{0,4},{4,0},{8,12},{12,8},{1,5},{5,1},{9,13},{13,9},{2,6},{6,2},{1... | collective-permute-start | bytes 393224 | tf_op jit(solution)/shard_map/ppermute | solution.py:394
  9.4 9.3 %collective-permute-start.2 = (bf16[512,128]{1,0:T(8,128)(2,1)S(1)}, bf16[512,128]{1,0:T(8,128)(2,1)S(1)}, u32[]{:S(2)}, u32[]{:S(2)}) collective-permute-start(bf16[512,128]{1,0:T(8,128)(2,1)S(1)} %shard_map.66.refs_3_), channel_id=1, source_target_pairs={{4,8},{8,4},{5,9},{9,5},{6,10},{10,6},{7,11},{11,7},{20,24},{24,20... | collective-permute-start | bytes 393224 | tf_op jit(solution)/shard_map/ppermute | solution.py:395
  13.1 5.6 %collective-permute-start.4 = (bf16[512,128]{1,0:T(8,128)(2,1)S(1)}, bf16[512,128]{1,0:T(8,128)(2,1)S(1)}, u32[]{:S(2)}, u32[]{:S(2)}) collective-permute-start(bf16[512,128]{1,0:T(8,128)(2,1)S(1)} %collective-permute-done.3.refs_6_), channel_id=1, source_target_pairs={{0,4},{4,0},{8,12},{12,8},{1,5},{5,1},{9,13},{13,9},{2,6},{6,2},{1... | collective-permute-start | bytes 393224 | tf_op jit(solution)/shard_map/ppermute | solution.py:394
  14.4 5.7 %collective-permute-start.5 = (bf16[512,128]{1,0:T(8,128)(2,1)S(1)}, bf16[512,128]{1,0:T(8,128)(2,1)S(1)}, u32[]{:S(2)}, u32[]{:S(2)}) collective-permute-start(bf16[512,128]{1,0:T(8,128)(2,1)S(1)} %collective-permute-done.3.refs_6_), channel_id=1, source_target_pairs={{4,8},{8,4},{5,9},{9,5},{6,10},{10,6},{7,11},{11,7},{20,24},{24,20... | collective-permute-start | bytes 393224 | tf_op jit(solution)/shard_map/ppermute | solution.py:395
  22.1 5.3 %collective-permute-start.7 = (bf16[2,512,128]{2,1,0:T(8,128)(2,1)S(1)}, bf16[2,512,128]{2,1,0:T(8,128)(2,1)S(1)}, u32[]{:S(2)}, u32[]{:S(2)}) collective-permute-start(bf16[2,512,128]{2,1,0:T(8,128)(2,1)S(1)} %shard_map.69.refs_4_), channel_id=1, source_target_pairs={{0,4},{4,0},{8,12},{12,8},{1,5},{5,1},{9,13},{13,9},{2,6},{6,2},{1... | collective-permute-start | bytes 786440 | tf_op jit(solution)/shard_map/ppermute | solution.py:394
  22.2 7.4 %collective-permute-start.8 = (bf16[2,512,128]{2,1,0:T(8,128)(2,1)S(1)}, bf16[2,512,128]{2,1,0:T(8,128)(2,1)S(1)}, u32[]{:S(2)}, u32[]{:S(2)}) collective-permute-start(bf16[2,512,128]{2,1,0:T(8,128)(2,1)S(1)} %shard_map.69.refs_4_), channel_id=1, source_target_pairs={{4,8},{8,4},{5,9},{9,5},{6,10},{10,6},{7,11},{11,7},{20,24},{24,20... | collective-permute-start | bytes 786440 | tf_op jit(solution)/shard_map/ppermute | solution.py:395
  31.5 4.5 %collective-permute-start.9 = (bf16[512,128]{1,0:T(8,128)(2,1)S(1)}, bf16[512,128]{1,0:T(8,128)(2,1)S(1)}, u32[]{:S(2)}, u32[]{:S(2)}) collective-permute-start(bf16[512,128]{1,0:T(8,128)(2,1)S(1)} %get-tuple-element.27), channel_id=1, source_target_pairs={{0,2},{2,0},{1,3},{3,1},{4,6},{6,4},{5,7},{7,5},{8,10},{10,8},{9,1... | collective-permute-start | bytes 393224 | tf_op jit(solution)/shard_map/ppermute | solution.py:384
  31.8 10.4 %collective-permute-start.12 = (bf16[512,128]{1,0:T(8,128)(2,1)S(1)}, bf16[512,128]{1,0:T(8,128)(2,1)S(1)}, u32[]{:S(2)}, u32[]{:S(2)}) collective-permute-start(bf16[512,128]{1,0:T(8,128)(2,1)S(1)} %get-tuple-element.28.piece_ref), channel_id=1, source_target_pairs={{0,1},{1,0},{2,3},{3,2},{4,5},{5,4},{6,7},{7,6},{8,9},{9,8},{10,11... | collective-permute-start | bytes 393224 | tf_op jit(solution)/shard_map/ppermute | solution.py:380
  35.9 6.9 %collective-permute-start.10 = (bf16[512,128]{1,0:T(8,128)(2,1)S(1)}, bf16[512,128]{1,0:T(8,128)(2,1)S(1)}, u32[]{:S(2)}, u32[]{:S(2)}) collective-permute-start(bf16[512,128]{1,0:T(8,128)(2,1)S(1)} %collective-permute-done.9.piece_ref), channel_id=1, source_target_pairs={{0,1},{1,0},{2,3},{3,2},{4,5},{5,4},{6,7},{7,6},{8,9},{9,8},{10,11... | collective-permute-start | bytes 393224 | tf_op jit(solution)/shard_map/ppermute | solution.py:380

commit v3 on v2

--- a/solution.py
+++ b/solution.py
@@ -10,6 +10,7 @@
 GROUP = 48
 ALIGN = 16
 UNROLL = 3
+FINAL_CHUNKS = 4
 F32 = jnp.float32
 BF16 = jnp.bfloat16
 VMEM = pl.BlockSpec(memory_space=pltpu.VMEM)
@@ -169,23 +170,15 @@
     make_bands(seg, starts_ref, table_ref, bands_ref)
 
 
-def echo_body(parts, cell_count, time_any, echo_any, perm_ref, *rest):
-    outs, (time_ref, echo_ref, tmp_ref, sems) = rest[:parts], rest[parts:]
+def echo_body(parts, cell_count, time_ref, echo_ref, perm_ref, *rest):
+    outs, tmp_ref = rest[:parts], rest[parts]
     bins = perm_ref.shape[1]
     owner = lax.axis_index("az") * parts + lax.axis_index("rg")
-    loads = [
-        pltpu.make_async_copy(time_any, time_ref, sems.at[0]),
-        pltpu.make_async_copy(echo_any, echo_ref, sems.at[1]),
-    ]
-    for load in loads:
-        load.start()
-    loads[0].wait()
     local = (time_ref[...] - owner * cell_count).astype(F32)
     slots = local.shape[1]
     hits = column_of(local) == iota((slots, cell_count), 1).astype(F32)
     place = hits.astype(BF16)
     occupied = jnp.sum(hits.astype(F32), axis=0, keepdims=True)
-    loads[1].wait()
     gridded = split_complex(tmp_ref, mm(echo_ref[...], place))
     for step in range(parts):
         moved = mm(perm_ref[step], gridded).astype(BF16)
@@ -322,20 +315,26 @@
         outs[step][...] = sum_ref[part_of(parts, step)].astype(BF16)
 
 
-def turn_body(parts, matrix_ref, perm_ref, moved_ref, out_ref, sorted_ref):
+def turn_own_body(parts, matrix_ref, perm_ref, out_ref, sorted_ref):
     def store(side, rows, value):
         sorted_ref[side, rows, :] = value
 
     columns = half_columns(matrix_ref.shape[1], lax.axis_index("cplx"))
     sorted_matrix(parts, matrix_ref, perm_ref, columns, store)
     for side in range(2):
-        out_ref[0, side] = sorted_ref[side].T
-        out_ref[1, side] = moved_ref[side].T
-
-
-def gradient_body(parts, source, step, begun, final, piece_ref, turned_ref, *refs):
-    out_ref = refs[-1]
-    rows_own = turned_ref.shape[2]
+        out_ref[side] = sorted_ref[side].T
+
+
+def turn_other_body(moved_ref, out_ref):
+    for side in range(2):
+        out_ref[side] = moved_ref[side].T
+
+
+def gradient_body(parts, step, begun, final, piece_ref, turned_ref, *refs):
+    refs = list(refs)
+    begun_ref = refs.pop(0) if begun else None
+    out_ref = refs[0]
+    rows_own = turned_ref.shape[1]
     cells = piece_ref.shape[-1]
     bins = rows_own // parts
     pieces = [piece_ref[...]] if len(piece_ref.shape) == 2 else [piece_ref[n] for n in range(parts)]
@@ -346,16 +345,29 @@
         columns = slice(None)
     else:
         columns = pl.ds(pl.multiple_of(part_of(parts, step) * bins, bins), bins)
-    real, imag = [mm(turned_ref[source, side, :, columns], both) for side in range(2)]
-    total = [real[:, :cells] + imag[:, cells:], real[:, cells:] - imag[:, :cells]]
-    if begun:
-        total = [total[0] + refs[0][:, :cells], total[1] + refs[0][:, cells:]]
-    if final:
-        out_ref[pl.ds(0, rows_own, stride=2), :] = total[0]
-        out_ref[pl.ds(1, rows_own, stride=2), :] = total[1]
-    else:
-        out_ref[:, :cells] = total[0]
-        out_ref[:, cells:] = total[1]
+    chunks = FINAL_CHUNKS if final else 1
+    size = rows_own // chunks
+    stores = []
+    for chunk in range(chunks):
+        rows = slice(chunk * size, (chunk + 1) * size)
+        real, imag = [mm(turned_ref[side, rows, columns], both) for side in range(2)]
+        total = [real[:, :cells] + imag[:, cells:], real[:, cells:] - imag[:, :cells]]
+        if begun:
+            total = [total[0] + begun_ref[rows, :cells], total[1] + begun_ref[rows, cells:]]
+        if final:
+            space_ref, sems = refs[1:]
+            space_ref[pl.ds(2 * chunk * size, size, stride=2), :] = total[0]
+            space_ref[pl.ds(2 * chunk * size + 1, size, stride=2), :] = total[1]
+            where = pl.ds(2 * chunk * size, 2 * size)
+            stores.append(
+                pltpu.make_async_copy(space_ref.at[where, :], out_ref.at[where, :], sems.at[chunk])
+            )
+            stores[-1].start()
+        else:
+            out_ref[rows, :cells] = total[0]
+            out_ref[rows, cells:] = total[1]
+    for store in stores:
+        store.wait()
 
 
 def swap_pairs(count, first):
@@ -444,19 +456,12 @@
     echo_pieces = call(
         functools.partial(echo_body, parts, cells),
         [struct((2 * bins + 16, cells), BF16)] * parts,
-        [in_hbm] * 2 + [VMEM],
-        [
-            pltpu.VMEM((1, slot_time.shape[0]), jnp.int32),
-            pltpu.VMEM((2 * rows_own, echoes.shape[2]), BF16),
-            split_space,
-            pltpu.SemaphoreType.DMA((2,)),
-        ],
+        [VMEM] * 3,
+        [split_space],
         flops=4 * rows_own * rows_own * cells,
     )(
-        *stay(
-            slot_time.reshape(1, slot_time.shape[0]),
-            echoes.reshape(2 * rows_own, echoes.shape[2]),
-        ),
+        slot_time.reshape(1, slot_time.shape[0]),
+        echoes.reshape(2 * rows_own, echoes.shape[2]),
         perms,
     )
     echo_own = share(echo_pieces)
@@ -501,13 +506,15 @@
         [table_space],
         flops=10**9,
     )(tiles[0], filter_bank)
-    turned = call(
-        functools.partial(turn_body, parts),
-        struct((2, 2, rows_own, rows_own), BF16),
-        [VMEM] * 3,
-        [pltpu.VMEM((2, rows_own, rows_own), BF16)],
+    square = struct((2, rows_own, rows_own), BF16)
+    turned_own = call(
+        functools.partial(turn_own_body, parts),
+        square,
+        [VMEM] * 2,
+        [pltpu.VMEM(square.shape, BF16)],
         flops=4 * rows_own**3,
-    )(matrix, perms, moved)
+    )(matrix, perms)
+    turned_other = call(turn_other_body, square, [VMEM], flops=10**8)(moved)
     back = call(
         functools.partial(adjoint_body, parts, halo, group),
         [piece] * parts,
@@ -523,12 +530,17 @@
     for number in range(len(back_own)):
         for source, x in enumerate((back_own[number], back_other[number])):
             final = source == 1 and number == len(back_own) - 1
-            args = [x, turned] + ([] if total is None else [total])
+            begun = total is not None
+            args = [x, (turned_own, turned_other)[source]] + ([total] if begun else [])
+            shape = (2 * rows_own, cells) if final else (rows_own, 2 * cells)
+            spaces = [pltpu.VMEM(shape, F32), pltpu.SemaphoreType.DMA((FINAL_CHUNKS,))]
             total = call(
-                functools.partial(gradient_body, parts, source, number, total is not None, final),
-                struct((2 * rows_own, cells) if final else (rows_own, 2 * cells), F32),
+                functools.partial(gradient_body, parts, number, begun, final),
+                struct(shape, F32),
                 [VMEM] * len(args),
+                spaces if final else (),
                 flops=8 * rows_own * bins * 2 * cells,
+                out_specs=in_hbm if final else None,
             )(*args)
     return total.reshape(rows_own, 2, cells)
 

time: 44.1 us -> 43.3 us (0.982)
  waiting for transfers between devices: 7.24 us -> 6.45 us
  Pallas kernels: 16.8 us -> 16.1 us
  starting transfers between devices: 19.6 us -> 20.3 us
    pallas_call x1, Pallas kernels: 1.48 us -> 0.59 us  [on_device(): call(functools.partial(echo_body, parts, cells), [struct((2 * bins + 16,...]
    ppermute x3, starting transfers between devices: 1.22 us -> 1.95 us  [share(): return [pieces[0], lax.ppermute(pieces[1], 'rg', flip)]]
    ppermute x4, waiting for transfers between devices: 0.71 us -> 0.01 us  [halves(): return lax.ppermute(x, 'cplx', flip)]
    pallas_call x5 -> x6, Pallas kernels: 3.03 us -> 3.25 us  [the longest x4 1.91 us: on_device(): call(functools.partial(gradient_body, parts, number, begun, final), struc...]
  transfers between devices with their start and end apart: 13 -> 13, of which waited for: 5 -> 4; matrix products, arithmetic and copies ran while one was open for 0% -> 0% of each run, Pallas kernels for 29% -> 35%
where the time goes in v3:
time: 43.3 us; the launch traced here: 43.1 us
  starting transfers between devices  20.3 us (47%)
  Pallas kernels  16.1 us (37%)
  waiting for transfers between devices  6.45 us (15%)
    ppermute x4, starting transfers between devices, halves(): return lax.ppermute(x, 'cplx', flip)  9.88 us
    ppermute x3, starting transfers between devices, sides(): odd = lax.ppermute(to_odd, 'az', odd_pairs)  5.77 us
    ppermute x3, waiting for transfers between devices, sides(): odd = lax.ppermute(to_odd, 'az', odd_pairs)  3.62 us
    ppermute x3, starting transfers between devices, sides(): even = lax.ppermute(to_even, 'az', even_pairs)  2.73 us
    pallas_call x1, Pallas kernels, on_device(): call(functools.partial(prep_body, parts, group), (struct((bank + 2,), jnp...  2.34 us
    pallas_call x1, Pallas kernels, on_device(): call(functools.partial(forward_bands_body, cells), bands_struct, [SMEM, V...  2.31 us
    pallas_call x1, Pallas kernels, on_device(): call(functools.partial(adjoint_bands_body, cells), bands_struct, [SMEM, V...  2.16 us
    pallas_call x1, Pallas kernels, on_device(): call(functools.partial(forward_body, parts, halo, group, names), struct((...  1.95 us
  transfers between devices with their start and end apart: 13, of which 4 were waited for; matrix products, arithmetic and copies ran while one was open for 0% of the time, Pallas kernels for 35%

profile of v3, /device:TPU:19, one launch (start us, length us, event | category | flops | bytes accessed | tf_op | source)
XLA Modules:
  0.0 43.1 jit_solution(9599080686915337639)
XLA Ops:
  0.0 0.0 copy-start.2
  0.0 0.0 copy-start
  0.0 0.7 %collective-permute-start = (bf16[1024,128]{1,0:T(8,128)(2,1)}, bf16[1024,128]{1,0:T(8,128)(2,1)S(1)}, u32[]{:S(2)}, u32[]{:S(2)}) collective-permute-start(bf16[1024,128]{1,0:T(8,128)(2,1)} %bitcast.7), channel_id=1, source_target_pairs={{0,1},{1,0},{2,3},{3,2},{4,5},{5,4},{6,7},{7,6},{8,9},{9,8},{10,11... | collective-permute-start | bytes 786440 | tf_op jit(solution)/shard_map/ppermute | solution.py:392
  0.7 0.0 copy-start.1
  0.7 2.3 %shard_map.64 = (s32[18]{0:T(128)S(1)}, s32[40]{0:T(128)S(1)}, s32[40]{0:T(128)S(1)}, bf16[2,256,512]{2,1,0:T(8,128)(2,1)S(1)}, bf16[2,512,1024]{2,1,0:T(8,128)(2,1)S(1)}, /*index=5*/f32[512,256]{1,0:T(8,128)S(1)}) custom-call(s32[1,1024]{1,0:T(1,128)} %bitcast.9, bf16[1024,128]{1,0:T(8,128)(2,1)} %bitcast.8, bf16[2,512,1024]{2,1,0:T(8,128)(2,1)} %matrix_any.1), custom_call_target="tpu_custom_call" | custom-call | flops 268435456 | bytes 3146120 | tf_op jit(solution)/shard_map/pallas_call | solution.py:422
  3.0 0.7 %shard_map.72 = bf16[2,512,512]{2,1,0:T(8,128)(2,1)S(1)} custom-call(bf16[2,512,1024]{2,1,0:T(8,128)(2,1)S(1)} %get-tuple-element.20.matrix_ref, bf16[2,256,512]{2,1,0:T(8,128)(2,1)S(1)} %get-tuple-element.21.perm_ref), custom_call_target="tpu_custom_call" | custom-call | flops 536870912 | bytes 1048576 | tf_op jit(solution)/shard_map/pallas_call | solution.py:482
  3.8 0.1 collective-permute-start.11
  3.9 0.0 copy-done.2
  3.9 0.0 copy-done
  3.9 0.6 %shard_map.68 = (bf16[528,128]{1,0:T(8,128)(2,1)S(1)}, bf16[528,128]{1,0:T(8,128)(2,1)S(1)}) custom-call(s32[1,128]{1,0:T(1,128)S(1)} %bitcast.6, bf16[1024,128]{1,0:T(8,128)(2,1)S(1)} %bitcast.5, bf16[2,256,512]{2,1,0:T(8,128)(2,1)S(1)} %get-tuple-element.21.perm_ref), custom_call_target="tpu_custom_call" | custom-call | flops 134217728 | bytes 270336 | tf_op jit(solution)/shard_map/pallas_call | solution.py:456
  4.5 0.3 collective-permute-start.6
  4.8 0.0 collective-permute-done.image_ref
  4.8 0.7 %shard_map.65 = (bf16[512,128]{1,0:T(8,128)(2,1)S(1)}, bf16[512,256]{1,0:T(8,128)(2,1)S(1)}) custom-call(bf16[1024,128]{1,0:T(8,128)(2,1)S(1)} %collective-permute-done.image_ref, bf16[2,512,1024]{2,1,0:T(8,128)(2,1)S(1)} %get-tuple-element.20.matrix_ref, bf16[2,256,512]{2,1,0:T(8,128)(2,1)S(1)} %get-tuple-element.21.perm_ref, ...), custom_call_target="tpu_custom_call" | custom-call | flops 268435456 | bytes 393216 | tf_op jit(solution)/shard_map/pallas_call | solution.py:444
  5.5 1.3 %collective-permute-start.3 = (bf16[512,128]{1,0:T(8,128)(2,1)S(1)}, bf16[512,128]{1,0:T(8,128)(2,1)S(1)}, u32[]{:S(2)}, u32[]{:S(2)}) collective-permute-start(bf16[512,128]{1,0:T(8,128)(2,1)S(1)} %get-tuple-element.24), channel_id=1, source_target_pairs={{0,2},{2,0},{1,3},{3,1},{4,6},{6,4},{5,7},{7,5},{8,10},{10,8},{9,1... | collective-permute-start | bytes 393224 | tf_op jit(solution)/shard_map/ppermute | solution.py:396
  6.8 0.2 shard_map.66.refs_3_
  7.0 1.4 %collective-permute-start.1 = (bf16[512,128]{1,0:T(8,128)(2,1)S(1)}, bf16[512,128]{1,0:T(8,128)(2,1)S(1)}, u32[]{:S(2)}, u32[]{:S(2)}) collective-permute-start(bf16[512,128]{1,0:T(8,128)(2,1)S(1)} %shard_map.66.refs_3_), channel_id=1, source_target_pairs={{0,4},{4,0},{8,12},{12,8},{1,5},{5,1},{9,13},{13,9},{2,6},{6,2},{1... | collective-permute-start | bytes 393224 | tf_op jit(solution)/shard_map/ppermute | solution.py:406
  8.4 1.9 %collective-permute-start.2 = (bf16[512,128]{1,0:T(8,128)(2,1)S(1)}, bf16[512,128]{1,0:T(8,128)(2,1)S(1)}, u32[]{:S(2)}, u32[]{:S(2)}) collective-permute-start(bf16[512,128]{1,0:T(8,128)(2,1)S(1)} %shard_map.66.refs_3_), channel_id=1, source_target_pairs={{4,8},{8,4},{5,9},{9,5},{6,10},{10,6},{7,11},{11,7},{20,24},{24,20... | collective-permute-start | bytes 393224 | tf_op jit(solution)/shard_map/ppermute | solution.py:407
  10.3 1.7 %collective-permute-done.3.refs_6_ = bf16[512,128]{1,0:T(8,128)(2,1)S(1)} collective-permute-done((bf16[512,128]{1,0:T(8,128)(2,1)S(1)}, bf16[512,128]{1,0:T(8,128)(2,1)S(1)}, u32[]{:S(2)}, u32[]{:S(2)}) %collective-permute-start.3) | collective-permute-done | bytes 131104 | tf_op jit(solution)/shard_map/ppermute | solution.py:396
  12.0 1.3 %collective-permute-start.4 = (bf16[512,128]{1,0:T(8,128)(2,1)S(1)}, bf16[512,128]{1,0:T(8,128)(2,1)S(1)}, u32[]{:S(2)}, u32[]{:S(2)}) collective-permute-start(bf16[512,128]{1,0:T(8,128)(2,1)S(1)} %collective-permute-done.3.refs_6_), channel_id=1, source_target_pairs={{0,4},{4,0},{8,12},{12,8},{1,5},{5,1},{9,13},{13,9},{2,6},{6,2},{1... | collective-permute-start | bytes 393224 | tf_op jit(solution)/shard_map/ppermute | solution.py:406
  13.3 0.0 collective-permute-done.6.refs_11_
  13.3 1.9 %collective-permute-start.5 = (bf16[512,128]{1,0:T(8,128)(2,1)S(1)}, bf16[512,128]{1,0:T(8,128)(2,1)S(1)}, u32[]{:S(2)}, u32[]{:S(2)}) collective-permute-start(bf16[512,128]{1,0:T(8,128)(2,1)S(1)} %collective-permute-done.3.refs_6_), channel_id=1, source_target_pairs={{4,8},{8,4},{5,9},{9,5},{6,10},{10,6},{7,11},{11,7},{20,24},{24,20... | collective-permute-start | bytes 393224 | tf_op jit(solution)/shard_map/ppermute | solution.py:407
  15.2 0.0 copy-done.1
  15.2 2.3 %shard_map.67.refs_9_ = bf16[16,640,256]{2,1,0:T(8,128)(2,1)S(1)} custom-call(s32[18]{0:T(128)S(1)} %get-tuple-element.17.starts_ref.refs_0_, bf16[16,2,512]{2,1,0:T(2,128)(2,1)S(1)} %copy-done.1), custom_call_target="tpu_custom_call" | custom-call | flops 1000000000 | bytes 5242880 | tf_op jit(solution)/shard_map/pallas_call | solution.py:475
  17.6 0.0 collective-permute-done.1.refs_4_
  17.6 0.0 collective-permute-done.2.refs_5_
  17.6 0.0 collective-permute-done.4.refs_7_
  17.6 1.4 %collective-permute-done.5.refs_8_ = bf16[512,128]{1,0:T(8,128)(2,1)S(1)} collective-permute-done((bf16[512,128]{1,0:T(8,128)(2,1)S(1)}, bf16[512,128]{1,0:T(8,128)(2,1)S(1)}, u32[]{:S(2)}, u32[]{:S(2)}) %collective-permute-start.5) | collective-permute-done | bytes 131104 | tf_op jit(solution)/shard_map/ppermute | solution.py:407
  19.0 1.9 %shard_map.69.refs_4_ = bf16[2,512,128]{2,1,0:T(8,128)(2,1)S(1)} custom-call(s32[18]{0:T(128)S(1)} %get-tuple-element.17.starts_ref.refs_0_, s32[40]{0:T(128)S(1)} %get-tuple-element.18.refs_1_, s32[40]{0:T(128)S(1)} %get-tuple-element.19.refs_2_, bf16[512,128]{1,0:T(8,128)(2,1)S(1)} %shard_map.66.refs_3_, ...), custom_call_target="tpu_custom_call" | custom-call | flops 335544320 | bytes 262144 | tf_op jit(solution)/shard_map/pallas_call | solution.py:494
  21.0 0.1 collective-permute-start.7
  21.1 2.0 %collective-permute-start.8 = (bf16[2,512,128]{2,1,0:T(8,128)(2,1)S(1)}, bf16[2,512,128]{2,1,0:T(8,128)(2,1)S(1)}, u32[]{:S(2)}, u32[]{:S(2)}) collective-permute-start(bf16[2,512,128]{2,1,0:T(8,128)(2,1)S(1)} %shard_map.69.refs_4_), channel_id=1, source_target_pairs={{4,8},{8,4},{5,9},{9,5},{6,10},{10,6},{7,11},{11,7},{20,24},{24,20... | collective-permute-start | bytes 786440 | tf_op jit(solution)/shard_map/ppermute | solution.py:407
  23.0 2.2 %shard_map.70.refs_6_ = bf16[16,640,256]{2,1,0:T(8,128)(2,1)S(1)} custom-call(s32[18]{0:T(128)S(1)} %get-tuple-element.17.starts_ref.refs_0_, bf16[16,2,512]{2,1,0:T(2,128)(2,1)S(1)} %copy-done.1), custom_call_target="tpu_custom_call" | custom-call | flops 1000000000 | bytes 5242880 | tf_op jit(solution)/shard_map/pallas_call | solution.py:502
  25.2 1.1 %collective-permute-done.7.refs_3_ = bf16[2,512,128]{2,1,0:T(8,128)(2,1)S(1)} collective-permute-done((bf16[2,512,128]{2,1,0:T(8,128)(2,1)S(1)}, bf16[2,512,128]{2,1,0:T(8,128)(2,1)S(1)}, u32[]{:S(2)}, u32[]{:S(2)}) %collective-permute-start.7) | collective-permute-done | bytes 262176 | tf_op jit(solution)/shard_map/ppermute | solution.py:406
  26.3 2.2 %collective-permute-done.8.refs_5_ = bf16[2,512,128]{2,1,0:T(8,128)(2,1)S(1)} collective-permute-done((bf16[2,512,128]{2,1,0:T(8,128)(2,1)S(1)}, bf16[2,512,128]{2,1,0:T(8,128)(2,1)S(1)}, u32[]{:S(2)}, u32[]{:S(2)}) %collective-permute-start.8) | collective-permute-done | bytes 262176 | tf_op jit(solution)/shard_map/ppermute | solution.py:407
  28.5 1.9 %shard_map.71 = (bf16[512,128]{1,0:T(8,128)(2,1)S(1)}, bf16[512,128]{1,0:T(8,128)(2,1)S(1)}) custom-call(s32[18]{0:T(128)S(1)} %get-tuple-element.17.starts_ref.refs_0_, s32[40]{0:T(128)S(1)} %get-tuple-element.18.refs_1_, s32[40]{0:T(128)S(1)} %get-tuple-element.19.refs_2_, bf16[2,512,128]{2,1,0:T(8,128)(2,1)S(1)} %collective-permute-done.7.refs_3_, ...), custom_call_target="tpu_custom_call" | custom-call | flops 335544320 | bytes 262144 | tf_op jit(solution)/shard_map/pallas_call | solution.py:518
  30.4 0.3 collective-permute-start.9
  30.7 4.2 %collective-permute-start.12 = (bf16[512,128]{1,0:T(8,128)(2,1)S(1)}, bf16[512,128]{1,0:T(8,128)(2,1)S(1)}, u32[]{:S(2)}, u32[]{:S(2)}) collective-permute-start(bf16[512,128]{1,0:T(8,128)(2,1)S(1)} %get-tuple-element.28.piece_ref), channel_id=1, source_target_pairs={{0,1},{1,0},{2,3},{3,2},{4,5},{5,4},{6,7},{7,6},{8,9},{9,8},{10,11... | collective-permute-start | bytes 393224 | tf_op jit(solution)/shard_map/ppermute | solution.py:392
  34.9 0.0 collective-permute-done.9.piece_ref
  34.9 4.9 %collective-permute-start.10 = (bf16[512,128]{1,0:T(8,128)(2,1)S(1)}, bf16[512,128]{1,0:T(8,128)(2,1)S(1)}, u32[]{:S(2)}, u32[]{:S(2)}) collective-permute-start(bf16[512,128]{1,0:T(8,128)(2,1)S(1)} %collective-permute-done.9.piece_ref), channel_id=1, source_target_pairs={{0,1},{1,0},{2,3},{3,2},{4,5},{5,4},{6,7},{7,6},{8,9},{9,8},{10,11... | collective-permute-start | bytes 393224 | tf_op jit(solution)/shard_map/ppermute | solution.py:392
  39.8 1.0 %shard_map.74.turned_ref = bf16[2,512,512]{2,1,0:T(8,128)(2,1)S(1)} custom-call(bf16[2,512,1024]{2,1,0:T(8,128)(2,1)S(1)} %get-tuple-element.20.matrix_ref, bf16[2,256,512]{2,1,0:T(8,128)(2,1)S(1)} %get-tuple-element.21.perm_ref), custom_call_target="tpu_custom_call" | custom-call | flops 536870912 | bytes 1048576 | tf_op jit(solution)/shard_map/pallas_call | solution.py:510
  40.8 0.3 shard_map.75.refs_0_
  41.1 0.0 collective-permute-done.11.moved_ref
  41.1 0.3 shard_map.73.turned_ref
  41.5 0.0 collective-permute-done.12.piece_ref
  41.5 0.3 shard_map.76.refs_0_
  41.8 0.3 shard_map.77.refs_0_
  42.1 0.0 collective-permute-done.10.piece_ref
  42.1 1.0 %shard_map.78 = f32[1024,128]{1,0:T(8,128)} custom-call(bf16[512,128]{1,0:T(8,128)(2,1)S(1)} %collective-permute-done.10.piece_ref, bf16[2,512,512]{2,1,0:T(8,128)(2,1)S(1)} %shard_map.73.turned_ref, f32[512,256]{1,0:T(8,128)S(1)} %shard_map.77.refs_0_), custom_call_target="tpu_custom_call" | custom-call | flops 268435456 | bytes 524288 | tf_op jit(solution)/shard_map/pallas_call | solution.py:537
Async XLA Ops:
  0.0 3.9 %copy-start.2 = (s32[128]{0:T(128)S(1)}, s32[128]{0:T(128)}, u32[]{:S(2)}) copy-start(s32[128]{0:T(128)} %param.8) | copy-start | bytes 1540
  0.0 3.9 %copy-start = (bf16[512,2,128]{2,1,0:T(2,128)(2,1)S(1)}, bf16[512,2,128]{2,1,0:T(2,128)(2,1)}, u32[]{:S(2)}) copy-start(bf16[512,2,128]{2,1,0:T(2,128)(2,1)} %param.7) | copy-start | bytes 786436
  0.0 4.8 %collective-permute-start = (bf16[1024,128]{1,0:T(8,128)(2,1)}, bf16[1024,128]{1,0:T(8,128)(2,1)S(1)}, u32[]{:S(2)}, u32[]{:S(2)}) collective-permute-start(bf16[1024,128]{1,0:T(8,128)(2,1)} %bitcast.7), channel_id=1, source_target_pairs={{0,1},{1,0},{2,3},{3,2},{4,5},{5,4},{6,7},{7,6},{8,9},{9,8},{10,11... | collective-permute-start | bytes 786440 | tf_op jit(solution)/shard_map/ppermute | solution.py:392
  0.7 14.6 %copy-start.1 = (bf16[16,2,512]{2,1,0:T(2,128)(2,1)S(1)}, bf16[16,2,512]{2,1,0:T(2,128)(2,1)}, u32[]{:S(2)}) copy-start(bf16[16,2,512]{2,1,0:T(2,128)(2,1)} %bank_ref.3) | copy-start | bytes 98308
  3.8 37.4 %collective-permute-start.11 = (bf16[2,512,512]{2,1,0:T(8,128)(2,1)S(1)}, bf16[2,512,512]{2,1,0:T(8,128)(2,1)S(1)}, u32[]{:S(2)}, u32[]{:S(2)}) collective-permute-start(bf16[2,512,512]{2,1,0:T(8,128)(2,1)S(1)} %shard_map.72), channel_id=1, source_target_pairs={{0,1},{1,0},{2,3},{3,2},{4,5},{5,4},{6,7},{7,6},{8,9},{9,8},{10,11... | collective-permute-start | bytes 3145736 | tf_op jit(solution)/shard_map/ppermute | solution.py:392
  4.5 8.9 %collective-permute-start.6 = (bf16[528,128]{1,0:T(8,128)(2,1)S(1)}, bf16[528,128]{1,0:T(8,128)(2,1)S(1)}, u32[]{:S(2)}, u32[]{:S(2)}) collective-permute-start(bf16[528,128]{1,0:T(8,128)(2,1)S(1)} %get-tuple-element.26), channel_id=1, source_target_pairs={{0,2},{2,0},{1,3},{3,1},{4,6},{6,4},{5,7},{7,5},{8,10},{10,8},{9,1... | collective-permute-start | bytes 405512 | tf_op jit(solution)/shard_map/ppermute | solution.py:396
  5.5 6.5 %collective-permute-start.3 = (bf16[512,128]{1,0:T(8,128)(2,1)S(1)}, bf16[512,128]{1,0:T(8,128)(2,1)S(1)}, u32[]{:S(2)}, u32[]{:S(2)}) collective-permute-start(bf16[512,128]{1,0:T(8,128)(2,1)S(1)} %get-tuple-element.24), channel_id=1, source_target_pairs={{0,2},{2,0},{1,3},{3,1},{4,6},{6,4},{5,7},{7,5},{8,10},{10,8},{9,1... | collective-permute-start | bytes 393224 | tf_op jit(solution)/shard_map/ppermute | solution.py:396
  7.0 10.6 %collective-permute-start.1 = (bf16[512,128]{1,0:T(8,128)(2,1)S(1)}, bf16[512,128]{1,0:T(8,128)(2,1)S(1)}, u32[]{:S(2)}, u32[]{:S(2)}) collective-permute-start(bf16[512,128]{1,0:T(8,128)(2,1)S(1)} %shard_map.66.refs_3_), channel_id=1, source_target_pairs={{0,4},{4,0},{8,12},{12,8},{1,5},{5,1},{9,13},{13,9},{2,6},{6,2},{1... | collective-permute-start | bytes 393224 | tf_op jit(solution)/shard_map/ppermute | solution.py:406
  8.4 9.2 %collective-permute-start.2 = (bf16[512,128]{1,0:T(8,128)(2,1)S(1)}, bf16[512,128]{1,0:T(8,128)(2,1)S(1)}, u32[]{:S(2)}, u32[]{:S(2)}) collective-permute-start(bf16[512,128]{1,0:T(8,128)(2,1)S(1)} %shard_map.66.refs_3_), channel_id=1, source_target_pairs={{4,8},{8,4},{5,9},{9,5},{6,10},{10,6},{7,11},{11,7},{20,24},{24,20... | collective-permute-start | bytes 393224 | tf_op jit(solution)/shard_map/ppermute | solution.py:407
  12.0 5.6 %collective-permute-start.4 = (bf16[512,128]{1,0:T(8,128)(2,1)S(1)}, bf16[512,128]{1,0:T(8,128)(2,1)S(1)}, u32[]{:S(2)}, u32[]{:S(2)}) collective-permute-start(bf16[512,128]{1,0:T(8,128)(2,1)S(1)} %collective-permute-done.3.refs_6_), channel_id=1, source_target_pairs={{0,4},{4,0},{8,12},{12,8},{1,5},{5,1},{9,13},{13,9},{2,6},{6,2},{1... | collective-permute-start | bytes 393224 | tf_op jit(solution)/shard_map/ppermute | solution.py:406
  13.3 5.7 %collective-permute-start.5 = (bf16[512,128]{1,0:T(8,128)(2,1)S(1)}, bf16[512,128]{1,0:T(8,128)(2,1)S(1)}, u32[]{:S(2)}, u32[]{:S(2)}) collective-permute-start(bf16[512,128]{1,0:T(8,128)(2,1)S(1)} %collective-permute-done.3.refs_6_), channel_id=1, source_target_pairs={{4,8},{8,4},{5,9},{9,5},{6,10},{10,6},{7,11},{11,7},{20,24},{24,20... | collective-permute-start | bytes 393224 | tf_op jit(solution)/shard_map/ppermute | solution.py:407
  21.0 5.3 %collective-permute-start.7 = (bf16[2,512,128]{2,1,0:T(8,128)(2,1)S(1)}, bf16[2,512,128]{2,1,0:T(8,128)(2,1)S(1)}, u32[]{:S(2)}, u32[]{:S(2)}) collective-permute-start(bf16[2,512,128]{2,1,0:T(8,128)(2,1)S(1)} %shard_map.69.refs_4_), channel_id=1, source_target_pairs={{0,4},{4,0},{8,12},{12,8},{1,5},{5,1},{9,13},{13,9},{2,6},{6,2},{1... | collective-permute-start | bytes 786440 | tf_op jit(solution)/shard_map/ppermute | solution.py:406
  21.1 7.4 %collective-permute-start.8 = (bf16[2,512,128]{2,1,0:T(8,128)(2,1)S(1)}, bf16[2,512,128]{2,1,0:T(8,128)(2,1)S(1)}, u32[]{:S(2)}, u32[]{:S(2)}) collective-permute-start(bf16[2,512,128]{2,1,0:T(8,128)(2,1)S(1)} %shard_map.69.refs_4_), channel_id=1, source_target_pairs={{4,8},{8,4},{5,9},{9,5},{6,10},{10,6},{7,11},{11,7},{20,24},{24,20... | collective-permute-start | bytes 786440 | tf_op jit(solution)/shard_map/ppermute | solution.py:407
  30.4 4.6 %collective-permute-start.9 = (bf16[512,128]{1,0:T(8,128)(2,1)S(1)}, bf16[512,128]{1,0:T(8,128)(2,1)S(1)}, u32[]{:S(2)}, u32[]{:S(2)}) collective-permute-start(bf16[512,128]{1,0:T(8,128)(2,1)S(1)} %get-tuple-element.27), channel_id=1, source_target_pairs={{0,2},{2,0},{1,3},{3,1},{4,6},{6,4},{5,7},{7,5},{8,10},{10,8},{9,1... | collective-permute-start | bytes 393224 | tf_op jit(solution)/shard_map/ppermute | solution.py:396
  30.7 10.8 %collective-permute-start.12 = (bf16[512,128]{1,0:T(8,128)(2,1)S(1)}, bf16[512,128]{1,0:T(8,128)(2,1)S(1)}, u32[]{:S(2)}, u32[]{:S(2)}) collective-permute-start(bf16[512,128]{1,0:T(8,128)(2,1)S(1)} %get-tuple-element.28.piece_ref), channel_id=1, source_target_pairs={{0,1},{1,0},{2,3},{3,2},{4,5},{5,4},{6,7},{7,6},{8,9},{9,8},{10,11... | collective-permute-start | bytes 393224 | tf_op jit(solution)/shard_map/ppermute | solution.py:392
  34.9 7.2 %collective-permute-start.10 = (bf16[512,128]{1,0:T(8,128)(2,1)S(1)}, bf16[512,128]{1,0:T(8,128)(2,1)S(1)}, u32[]{:S(2)}, u32[]{:S(2)}) collective-permute-start(bf16[512,128]{1,0:T(8,128)(2,1)S(1)} %collective-permute-done.9.piece_ref), channel_id=1, source_target_pairs={{0,1},{1,0},{2,3},{3,2},{4,5},{5,4},{6,7},{7,6},{8,9},{9,8},{10,11... | collective-permute-start | bytes 393224 | tf_op jit(solution)/shard_map/ppermute | solution.py:392

commit v4 on v3

--- a/solution.py
+++ b/solution.py
@@ -246,12 +246,11 @@
     lax.fori_loop(0, lax.div(count + (UNROLL - 1), UNROLL), run, 0)
 
 
-def filtered(blocks_ref, bands, outputs, first, group, sign):
-    cells, bins = blocks_ref.shape[2], blocks_ref.shape[1] // 2
+def filtered(read, cells, bins, bands, outputs, first, group, sign):
     span = bands.shape[0] // cells
     rows = [
         jnp.concatenate(
-            [blocks_ref[block + at, pl.ds(side * bins + first, group), :] for at in range(span)], axis=1
+            [read(block + at, pl.ds(side * bins + first, group)) for at in range(span)], axis=1
         )
         for block in outputs
         for side in range(2)
@@ -267,17 +266,25 @@
     return results
 
 
-def filter_all(parts, group, tiles, blocks_ref, bands_ref, sum_ref, sign):
-    bins = blocks_ref.shape[1] // 2
+def filter_all(parts, group, tiles, read, bands_ref, sum_ref, sign):
+    bins, cells = sum_ref.shape[1] // 2, sum_ref.shape[2]
 
     def work(number, first, mask):
-        made = filtered(blocks_ref, bands_ref[number], range(parts), first, group, sign)
+        made = filtered(
+            read, cells, bins, bands_ref[number], range(parts), first, group, sign
+        )
         for block in range(parts):
             for side in range(2):
                 rows = pl.ds(side * bins + first, group)
                 sum_ref[block, rows, :] = jnp.where(mask, made[block][side], sum_ref[block, rows, :])
 
     filter_groups(*tiles, group, work)
+
+
+def run_views(here, parts, group, tiles, views, bands_ref, sum_ref, sign):
+    @pl.when(here)
+    def _():
+        filter_all(parts, group, tiles, lambda block, rows: views[block][rows, :], bands_ref, sum_ref, sign)
 
 
 def forward_body(parts, halo, group, names, *refs):
@@ -289,14 +296,17 @@
     bins = blocks_ref.shape[1] // 2
     even_base, odd_base = side_bases(parts, halo)
     base = {"even": even_base, "odd": odd_base, "own": halo}
-    fill_blocks(
-        blocks_ref,
-        [
-            (ref, base[side] + (part_of(parts, step) if parts == 2 else step))
-            for ref, (side, step) in zip(pieces, names)
-        ],
-    )
-    filter_all(parts, group, tiles, blocks_ref, bands_ref, sum_ref, 1.0)
+    if parts == 2:
+        for even in range(2):
+            for rg in range(2):
+                starts = {"even": (0, halo + parts)[even], "odd": (halo + parts, 0)[even], "own": halo}
+                views = {starts[side] + (rg ^ step): ref for ref, (side, step) in zip(pieces, names)}
+                here = (lax.rem(lax.axis_index("az"), 2) == 1 - even) & (lax.axis_index("rg") == rg)
+                run_views(here, parts, group, tiles, views, bands_ref, sum_ref, 1.0)
+    else:
+        fill_blocks(blocks_ref, [(ref, base[side] + step) for ref, (side, step) in zip(pieces, names)])
+        read = lambda block, rows: blocks_ref[block, rows, :]
+        filter_all(parts, group, tiles, read, bands_ref, sum_ref, 1.0)
     for step in range(parts):
         part = part_of(parts, step)
         echo = echoes[step][...] if len(echoes) > 1 else echoes[0][step]
@@ -309,8 +319,16 @@
     tiles, (even_ref, own_ref, odd_ref, bands_ref) = refs[:3], refs[3:7]
     outs, (blocks_ref, sum_ref) = refs[7 : 7 + parts], refs[7 + parts :]
     even_base, odd_base = side_bases(parts, halo)
-    fill_blocks(blocks_ref, [(even_ref, even_base), (own_ref, halo), (odd_ref, odd_base)])
-    filter_all(parts, group, tiles, blocks_ref, bands_ref, sum_ref, -1.0)
+    if parts == 2:
+        for even in range(2):
+            order = (even_ref, own_ref, odd_ref) if even == 0 else (odd_ref, own_ref, even_ref)
+            slabs = [ref.at[number] for ref in order for number in range(ref.shape[0])]
+            here = lax.rem(lax.axis_index("az"), 2) == 1 - even
+            run_views(here, parts, group, tiles, dict(enumerate(slabs)), bands_ref, sum_ref, -1.0)
+    else:
+        fill_blocks(blocks_ref, [(even_ref, even_base), (own_ref, halo), (odd_ref, odd_base)])
+        read = lambda block, rows: blocks_ref[block, rows, :]
+        filter_all(parts, group, tiles, read, bands_ref, sum_ref, -1.0)
     for step in range(parts):
         outs[step][...] = sum_ref[part_of(parts, step)].astype(BF16)
 

time: 43.3 us -> 43.3 us (level)
  no operation moved by 1% of the time
where the time goes in v4:
time: 43.3 us; the launch traced here: 43.1 us
  starting transfers between devices  20.4 us (47%)
  Pallas kernels  16.1 us (37%)
  waiting for transfers between devices  6.45 us (15%)
    ppermute x4, starting transfers between devices, halves(): return lax.ppermute(x, 'cplx', flip)  9.91 us
    ppermute x3, starting transfers between devices, sides(): odd = lax.ppermute(to_odd, 'az', odd_pairs)  5.77 us
    ppermute x3, waiting for transfers between devices, sides(): odd = lax.ppermute(to_odd, 'az', odd_pairs)  3.62 us
    ppermute x3, starting transfers between devices, sides(): even = lax.ppermute(to_even, 'az', even_pairs)  2.73 us
    pallas_call x1, Pallas kernels, on_device(): call(functools.partial(prep_body, parts, group), (struct((bank + 2,), jnp...  2.34 us
    pallas_call x1, Pallas kernels, on_device(): call(functools.partial(forward_bands_body, cells), bands_struct, [SMEM, V...  2.31 us
    pallas_call x1, Pallas kernels, on_device(): call(functools.partial(adjoint_bands_body, cells), bands_struct, [SMEM, V...  2.16 us
    ppermute x3, starting transfers between devices, share(): return [pieces[0], lax.ppermute(pieces[1], 'rg', flip)]  1.94 us
  transfers between devices with their start and end apart: 13, of which 4 were waited for; matrix products, arithmetic and copies ran while one was open for 0% of the time, Pallas kernels for 35%

profile of v4, /device:TPU:19, one launch (start us, length us, event | category | flops | bytes accessed | tf_op | source)
XLA Modules:
  0.0 43.1 jit_solution(2841935382054056369)
XLA Ops:
  0.0 0.0 copy-start.2
  0.0 0.0 copy-start
  0.0 0.7 %collective-permute-start = (bf16[1024,128]{1,0:T(8,128)(2,1)}, bf16[1024,128]{1,0:T(8,128)(2,1)S(1)}, u32[]{:S(2)}, u32[]{:S(2)}) collective-permute-start(bf16[1024,128]{1,0:T(8,128)(2,1)} %bitcast.7), channel_id=1, source_target_pairs={{0,1},{1,0},{2,3},{3,2},{4,5},{5,4},{6,7},{7,6},{8,9},{9,8},{10,11... | collective-permute-start | bytes 786440 | tf_op jit(solution)/shard_map/ppermute | solution.py:410
  0.7 0.0 copy-start.1
  0.7 2.3 %shard_map.64 = (s32[18]{0:T(128)S(1)}, s32[40]{0:T(128)S(1)}, s32[40]{0:T(128)S(1)}, bf16[2,256,512]{2,1,0:T(8,128)(2,1)S(1)}, bf16[2,512,1024]{2,1,0:T(8,128)(2,1)S(1)}, /*index=5*/f32[512,256]{1,0:T(8,128)S(1)}) custom-call(s32[1,1024]{1,0:T(1,128)} %bitcast.9, bf16[1024,128]{1,0:T(8,128)(2,1)} %bitcast.8, bf16[2,512,1024]{2,1,0:T(8,128)(2,1)} %matrix_any.1), custom_call_target="tpu_custom_call" | custom-call | flops 268435456 | bytes 3146120 | tf_op jit(solution)/shard_map/pallas_call | solution.py:440
  3.0 0.7 %shard_map.72 = bf16[2,512,512]{2,1,0:T(8,128)(2,1)S(1)} custom-call(bf16[2,512,1024]{2,1,0:T(8,128)(2,1)S(1)} %get-tuple-element.20.matrix_ref, bf16[2,256,512]{2,1,0:T(8,128)(2,1)S(1)} %get-tuple-element.21.perm_ref), custom_call_target="tpu_custom_call" | custom-call | flops 536870912 | bytes 1048576 | tf_op jit(solution)/shard_map/pallas_call | solution.py:500
  3.8 0.1 collective-permute-start.11
  3.9 0.0 copy-done.2
  3.9 0.0 copy-done
  3.9 0.6 %shard_map.68 = (bf16[528,128]{1,0:T(8,128)(2,1)S(1)}, bf16[528,128]{1,0:T(8,128)(2,1)S(1)}) custom-call(s32[1,128]{1,0:T(1,128)S(1)} %bitcast.6, bf16[1024,128]{1,0:T(8,128)(2,1)S(1)} %bitcast.5, bf16[2,256,512]{2,1,0:T(8,128)(2,1)S(1)} %get-tuple-element.21.perm_ref), custom_call_target="tpu_custom_call" | custom-call | flops 134217728 | bytes 270336 | tf_op jit(solution)/shard_map/pallas_call | solution.py:474
  4.5 0.3 collective-permute-start.6
  4.8 0.0 collective-permute-done.image_ref
  4.8 0.7 %shard_map.65 = (bf16[512,128]{1,0:T(8,128)(2,1)S(1)}, bf16[512,256]{1,0:T(8,128)(2,1)S(1)}) custom-call(bf16[1024,128]{1,0:T(8,128)(2,1)S(1)} %collective-permute-done.image_ref, bf16[2,512,1024]{2,1,0:T(8,128)(2,1)S(1)} %get-tuple-element.20.matrix_ref, bf16[2,256,512]{2,1,0:T(8,128)(2,1)S(1)} %get-tuple-element.21.perm_ref, ...), custom_call_target="tpu_custom_call" | custom-call | flops 268435456 | bytes 393216 | tf_op jit(solution)/shard_map/pallas_call | solution.py:462
  5.5 1.3 %collective-permute-start.3 = (bf16[512,128]{1,0:T(8,128)(2,1)S(1)}, bf16[512,128]{1,0:T(8,128)(2,1)S(1)}, u32[]{:S(2)}, u32[]{:S(2)}) collective-permute-start(bf16[512,128]{1,0:T(8,128)(2,1)S(1)} %get-tuple-element.24), channel_id=1, source_target_pairs={{0,2},{2,0},{1,3},{3,1},{4,6},{6,4},{5,7},{7,5},{8,10},{10,8},{9,1... | collective-permute-start | bytes 393224 | tf_op jit(solution)/shard_map/ppermute | solution.py:414
  6.8 0.2 shard_map.66.refs_3_
  7.0 1.4 %collective-permute-start.1 = (bf16[512,128]{1,0:T(8,128)(2,1)S(1)}, bf16[512,128]{1,0:T(8,128)(2,1)S(1)}, u32[]{:S(2)}, u32[]{:S(2)}) collective-permute-start(bf16[512,128]{1,0:T(8,128)(2,1)S(1)} %shard_map.66.refs_3_), channel_id=1, source_target_pairs={{0,4},{4,0},{8,12},{12,8},{1,5},{5,1},{9,13},{13,9},{2,6},{6,2},{1... | collective-permute-start | bytes 393224 | tf_op jit(solution)/shard_map/ppermute | solution.py:424
  8.4 1.9 %collective-permute-start.2 = (bf16[512,128]{1,0:T(8,128)(2,1)S(1)}, bf16[512,128]{1,0:T(8,128)(2,1)S(1)}, u32[]{:S(2)}, u32[]{:S(2)}) collective-permute-start(bf16[512,128]{1,0:T(8,128)(2,1)S(1)} %shard_map.66.refs_3_), channel_id=1, source_target_pairs={{4,8},{8,4},{5,9},{9,5},{6,10},{10,6},{7,11},{11,7},{20,24},{24,20... | collective-permute-start | bytes 393224 | tf_op jit(solution)/shard_map/ppermute | solution.py:425
  10.3 1.7 %collective-permute-done.3.refs_6_ = bf16[512,128]{1,0:T(8,128)(2,1)S(1)} collective-permute-done((bf16[512,128]{1,0:T(8,128)(2,1)S(1)}, bf16[512,128]{1,0:T(8,128)(2,1)S(1)}, u32[]{:S(2)}, u32[]{:S(2)}) %collective-permute-start.3) | collective-permute-done | bytes 131104 | tf_op jit(solution)/shard_map/ppermute | solution.py:414
  12.0 1.3 %collective-permute-start.4 = (bf16[512,128]{1,0:T(8,128)(2,1)S(1)}, bf16[512,128]{1,0:T(8,128)(2,1)S(1)}, u32[]{:S(2)}, u32[]{:S(2)}) collective-permute-start(bf16[512,128]{1,0:T(8,128)(2,1)S(1)} %collective-permute-done.3.refs_6_), channel_id=1, source_target_pairs={{0,4},{4,0},{8,12},{12,8},{1,5},{5,1},{9,13},{13,9},{2,6},{6,2},{1... | collective-permute-start | bytes 393224 | tf_op jit(solution)/shard_map/ppermute | solution.py:424
  13.3 0.0 collective-permute-done.6.refs_11_
  13.3 1.9 %collective-permute-start.5 = (bf16[512,128]{1,0:T(8,128)(2,1)S(1)}, bf16[512,128]{1,0:T(8,128)(2,1)S(1)}, u32[]{:S(2)}, u32[]{:S(2)}) collective-permute-start(bf16[512,128]{1,0:T(8,128)(2,1)S(1)} %collective-permute-done.3.refs_6_), channel_id=1, source_target_pairs={{4,8},{8,4},{5,9},{9,5},{6,10},{10,6},{7,11},{11,7},{20,24},{24,20... | collective-permute-start | bytes 393224 | tf_op jit(solution)/shard_map/ppermute | solution.py:425
  15.2 0.0 copy-done.1
  15.2 2.3 %shard_map.67.refs_9_ = bf16[16,640,256]{2,1,0:T(8,128)(2,1)S(1)} custom-call(s32[18]{0:T(128)S(1)} %get-tuple-element.17.starts_ref.refs_0_, bf16[16,2,512]{2,1,0:T(2,128)(2,1)S(1)} %copy-done.1), custom_call_target="tpu_custom_call" | custom-call | flops 1000000000 | bytes 5242880 | tf_op jit(solution)/shard_map/pallas_call | solution.py:493
  17.6 0.0 collective-permute-done.1.refs_4_
  17.6 0.0 collective-permute-done.2.refs_5_
  17.6 0.0 collective-permute-done.4.refs_7_
  17.6 1.4 %collective-permute-done.5.refs_8_ = bf16[512,128]{1,0:T(8,128)(2,1)S(1)} collective-permute-done((bf16[512,128]{1,0:T(8,128)(2,1)S(1)}, bf16[512,128]{1,0:T(8,128)(2,1)S(1)}, u32[]{:S(2)}, u32[]{:S(2)}) %collective-permute-start.5) | collective-permute-done | bytes 131104 | tf_op jit(solution)/shard_map/ppermute | solution.py:425
  19.0 1.9 %shard_map.69.refs_4_ = bf16[2,512,128]{2,1,0:T(8,128)(2,1)S(1)} custom-call(s32[18]{0:T(128)S(1)} %get-tuple-element.17.starts_ref.refs_0_, s32[40]{0:T(128)S(1)} %get-tuple-element.18.refs_1_, s32[40]{0:T(128)S(1)} %get-tuple-element.19.refs_2_, bf16[512,128]{1,0:T(8,128)(2,1)S(1)} %shard_map.66.refs_3_, ...), custom_call_target="tpu_custom_call" | custom-call | flops 335544320 | bytes 262144 | tf_op jit(solution)/shard_map/pallas_call | solution.py:512
  21.0 0.1 collective-permute-start.7
  21.0 2.0 %collective-permute-start.8 = (bf16[2,512,128]{2,1,0:T(8,128)(2,1)S(1)}, bf16[2,512,128]{2,1,0:T(8,128)(2,1)S(1)}, u32[]{:S(2)}, u32[]{:S(2)}) collective-permute-start(bf16[2,512,128]{2,1,0:T(8,128)(2,1)S(1)} %shard_map.69.refs_4_), channel_id=1, source_target_pairs={{4,8},{8,4},{5,9},{9,5},{6,10},{10,6},{7,11},{11,7},{20,24},{24,20... | collective-permute-start | bytes 786440 | tf_op jit(solution)/shard_map/ppermute | solution.py:425
  23.0 2.2 %shard_map.70.refs_6_ = bf16[16,640,256]{2,1,0:T(8,128)(2,1)S(1)} custom-call(s32[18]{0:T(128)S(1)} %get-tuple-element.17.starts_ref.refs_0_, bf16[16,2,512]{2,1,0:T(2,128)(2,1)S(1)} %copy-done.1), custom_call_target="tpu_custom_call" | custom-call | flops 1000000000 | bytes 5242880 | tf_op jit(solution)/shard_map/pallas_call | solution.py:520
  25.2 1.1 %collective-permute-done.7.refs_3_ = bf16[2,512,128]{2,1,0:T(8,128)(2,1)S(1)} collective-permute-done((bf16[2,512,128]{2,1,0:T(8,128)(2,1)S(1)}, bf16[2,512,128]{2,1,0:T(8,128)(2,1)S(1)}, u32[]{:S(2)}, u32[]{:S(2)}) %collective-permute-start.7) | collective-permute-done | bytes 262176 | tf_op jit(solution)/shard_map/ppermute | solution.py:424
  26.2 2.2 %collective-permute-done.8.refs_5_ = bf16[2,512,128]{2,1,0:T(8,128)(2,1)S(1)} collective-permute-done((bf16[2,512,128]{2,1,0:T(8,128)(2,1)S(1)}, bf16[2,512,128]{2,1,0:T(8,128)(2,1)S(1)}, u32[]{:S(2)}, u32[]{:S(2)}) %collective-permute-start.8) | collective-permute-done | bytes 262176 | tf_op jit(solution)/shard_map/ppermute | solution.py:425
  28.4 1.9 %shard_map.71 = (bf16[512,128]{1,0:T(8,128)(2,1)S(1)}, bf16[512,128]{1,0:T(8,128)(2,1)S(1)}) custom-call(s32[18]{0:T(128)S(1)} %get-tuple-element.17.starts_ref.refs_0_, s32[40]{0:T(128)S(1)} %get-tuple-element.18.refs_1_, s32[40]{0:T(128)S(1)} %get-tuple-element.19.refs_2_, bf16[2,512,128]{2,1,0:T(8,128)(2,1)S(1)} %collective-permute-done.7.refs_3_, ...), custom_call_target="tpu_custom_call" | custom-call | flops 335544320 | bytes 262144 | tf_op jit(solution)/shard_map/pallas_call | solution.py:536
  30.3 0.3 collective-permute-start.9
  30.7 4.2 %collective-permute-start.12 = (bf16[512,128]{1,0:T(8,128)(2,1)S(1)}, bf16[512,128]{1,0:T(8,128)(2,1)S(1)}, u32[]{:S(2)}, u32[]{:S(2)}) collective-permute-start(bf16[512,128]{1,0:T(8,128)(2,1)S(1)} %get-tuple-element.28.piece_ref), channel_id=1, source_target_pairs={{0,1},{1,0},{2,3},{3,2},{4,5},{5,4},{6,7},{7,6},{8,9},{9,8},{10,11... | collective-permute-start | bytes 393224 | tf_op jit(solution)/shard_map/ppermute | solution.py:410
  34.9 0.0 collective-permute-done.9.piece_ref
  34.9 4.9 %collective-permute-start.10 = (bf16[512,128]{1,0:T(8,128)(2,1)S(1)}, bf16[512,128]{1,0:T(8,128)(2,1)S(1)}, u32[]{:S(2)}, u32[]{:S(2)}) collective-permute-start(bf16[512,128]{1,0:T(8,128)(2,1)S(1)} %collective-permute-done.9.piece_ref), channel_id=1, source_target_pairs={{0,1},{1,0},{2,3},{3,2},{4,5},{5,4},{6,7},{7,6},{8,9},{9,8},{10,11... | collective-permute-start | bytes 393224 | tf_op jit(solution)/shard_map/ppermute | solution.py:410
  39.8 1.0 %shard_map.74.turned_ref = bf16[2,512,512]{2,1,0:T(8,128)(2,1)S(1)} custom-call(bf16[2,512,1024]{2,1,0:T(8,128)(2,1)S(1)} %get-tuple-element.20.matrix_ref, bf16[2,256,512]{2,1,0:T(8,128)(2,1)S(1)} %get-tuple-element.21.perm_ref), custom_call_target="tpu_custom_call" | custom-call | flops 536870912 | bytes 1048576 | tf_op jit(solution)/shard_map/pallas_call | solution.py:528
  40.8 0.3 shard_map.75.refs_0_
  41.1 0.0 collective-permute-done.11.moved_ref
  41.1 0.3 shard_map.73.turned_ref
  41.5 0.0 collective-permute-done.12.piece_ref
  41.5 0.3 shard_map.76.refs_0_
  41.8 0.3 shard_map.77.refs_0_
  42.1 0.0 collective-permute-done.10.piece_ref
  42.1 1.0 %shard_map.78 = f32[1024,128]{1,0:T(8,128)} custom-call(bf16[512,128]{1,0:T(8,128)(2,1)S(1)} %collective-permute-done.10.piece_ref, bf16[2,512,512]{2,1,0:T(8,128)(2,1)S(1)} %shard_map.73.turned_ref, f32[512,256]{1,0:T(8,128)S(1)} %shard_map.77.refs_0_), custom_call_target="tpu_custom_call" | custom-call | flops 268435456 | bytes 524288 | tf_op jit(solution)/shard_map/pallas_call | solution.py:555
Async XLA Ops:
  0.0 3.9 %copy-start.2 = (s32[128]{0:T(128)S(1)}, s32[128]{0:T(128)}, u32[]{:S(2)}) copy-start(s32[128]{0:T(128)} %param.8) | copy-start | bytes 1540
  0.0 3.9 %copy-start = (bf16[512,2,128]{2,1,0:T(2,128)(2,1)S(1)}, bf16[512,2,128]{2,1,0:T(2,128)(2,1)}, u32[]{:S(2)}) copy-start(bf16[512,2,128]{2,1,0:T(2,128)(2,1)} %param.7) | copy-start | bytes 786436
  0.0 4.8 %collective-permute-start = (bf16[1024,128]{1,0:T(8,128)(2,1)}, bf16[1024,128]{1,0:T(8,128)(2,1)S(1)}, u32[]{:S(2)}, u32[]{:S(2)}) collective-permute-start(bf16[1024,128]{1,0:T(8,128)(2,1)} %bitcast.7), channel_id=1, source_target_pairs={{0,1},{1,0},{2,3},{3,2},{4,5},{5,4},{6,7},{7,6},{8,9},{9,8},{10,11... | collective-permute-start | bytes 786440 | tf_op jit(solution)/shard_map/ppermute | solution.py:410
  0.7 14.6 %copy-start.1 = (bf16[16,2,512]{2,1,0:T(2,128)(2,1)S(1)}, bf16[16,2,512]{2,1,0:T(2,128)(2,1)}, u32[]{:S(2)}) copy-start(bf16[16,2,512]{2,1,0:T(2,128)(2,1)} %bank_ref.3) | copy-start | bytes 98308
  3.8 37.4 %collective-permute-start.11 = (bf16[2,512,512]{2,1,0:T(8,128)(2,1)S(1)}, bf16[2,512,512]{2,1,0:T(8,128)(2,1)S(1)}, u32[]{:S(2)}, u32[]{:S(2)}) collective-permute-start(bf16[2,512,512]{2,1,0:T(8,128)(2,1)S(1)} %shard_map.72), channel_id=1, source_target_pairs={{0,1},{1,0},{2,3},{3,2},{4,5},{5,4},{6,7},{7,6},{8,9},{9,8},{10,11... | collective-permute-start | bytes 3145736 | tf_op jit(solution)/shard_map/ppermute | solution.py:410
  4.5 8.9 %collective-permute-start.6 = (bf16[528,128]{1,0:T(8,128)(2,1)S(1)}, bf16[528,128]{1,0:T(8,128)(2,1)S(1)}, u32[]{:S(2)}, u32[]{:S(2)}) collective-permute-start(bf16[528,128]{1,0:T(8,128)(2,1)S(1)} %get-tuple-element.26), channel_id=1, source_target_pairs={{0,2},{2,0},{1,3},{3,1},{4,6},{6,4},{5,7},{7,5},{8,10},{10,8},{9,1... | collective-permute-start | bytes 405512 | tf_op jit(solution)/shard_map/ppermute | solution.py:414
  5.5 6.5 %collective-permute-start.3 = (bf16[512,128]{1,0:T(8,128)(2,1)S(1)}, bf16[512,128]{1,0:T(8,128)(2,1)S(1)}, u32[]{:S(2)}, u32[]{:S(2)}) collective-permute-start(bf16[512,128]{1,0:T(8,128)(2,1)S(1)} %get-tuple-element.24), channel_id=1, source_target_pairs={{0,2},{2,0},{1,3},{3,1},{4,6},{6,4},{5,7},{7,5},{8,10},{10,8},{9,1... | collective-permute-start | bytes 393224 | tf_op jit(solution)/shard_map/ppermute | solution.py:414
  7.0 10.6 %collective-permute-start.1 = (bf16[512,128]{1,0:T(8,128)(2,1)S(1)}, bf16[512,128]{1,0:T(8,128)(2,1)S(1)}, u32[]{:S(2)}, u32[]{:S(2)}) collective-permute-start(bf16[512,128]{1,0:T(8,128)(2,1)S(1)} %shard_map.66.refs_3_), channel_id=1, source_target_pairs={{0,4},{4,0},{8,12},{12,8},{1,5},{5,1},{9,13},{13,9},{2,6},{6,2},{1... | collective-permute-start | bytes 393224 | tf_op jit(solution)/shard_map/ppermute | solution.py:424
  8.4 9.2 %collective-permute-start.2 = (bf16[512,128]{1,0:T(8,128)(2,1)S(1)}, bf16[512,128]{1,0:T(8,128)(2,1)S(1)}, u32[]{:S(2)}, u32[]{:S(2)}) collective-permute-start(bf16[512,128]{1,0:T(8,128)(2,1)S(1)} %shard_map.66.refs_3_), channel_id=1, source_target_pairs={{4,8},{8,4},{5,9},{9,5},{6,10},{10,6},{7,11},{11,7},{20,24},{24,20... | collective-permute-start | bytes 393224 | tf_op jit(solution)/shard_map/ppermute | solution.py:425
  12.0 5.6 %collective-permute-start.4 = (bf16[512,128]{1,0:T(8,128)(2,1)S(1)}, bf16[512,128]{1,0:T(8,128)(2,1)S(1)}, u32[]{:S(2)}, u32[]{:S(2)}) collective-permute-start(bf16[512,128]{1,0:T(8,128)(2,1)S(1)} %collective-permute-done.3.refs_6_), channel_id=1, source_target_pairs={{0,4},{4,0},{8,12},{12,8},{1,5},{5,1},{9,13},{13,9},{2,6},{6,2},{1... | collective-permute-start | bytes 393224 | tf_op jit(solution)/shard_map/ppermute | solution.py:424
  13.3 5.7 %collective-permute-start.5 = (bf16[512,128]{1,0:T(8,128)(2,1)S(1)}, bf16[512,128]{1,0:T(8,128)(2,1)S(1)}, u32[]{:S(2)}, u32[]{:S(2)}) collective-permute-start(bf16[512,128]{1,0:T(8,128)(2,1)S(1)} %collective-permute-done.3.refs_6_), channel_id=1, source_target_pairs={{4,8},{8,4},{5,9},{9,5},{6,10},{10,6},{7,11},{11,7},{20,24},{24,20... | collective-permute-start | bytes 393224 | tf_op jit(solution)/shard_map/ppermute | solution.py:425
  21.0 5.3 %collective-permute-start.7 = (bf16[2,512,128]{2,1,0:T(8,128)(2,1)S(1)}, bf16[2,512,128]{2,1,0:T(8,128)(2,1)S(1)}, u32[]{:S(2)}, u32[]{:S(2)}) collective-permute-start(bf16[2,512,128]{2,1,0:T(8,128)(2,1)S(1)} %shard_map.69.refs_4_), channel_id=1, source_target_pairs={{0,4},{4,0},{8,12},{12,8},{1,5},{5,1},{9,13},{13,9},{2,6},{6,2},{1... | collective-permute-start | bytes 786440 | tf_op jit(solution)/shard_map/ppermute | solution.py:424
  21.0 7.4 %collective-permute-start.8 = (bf16[2,512,128]{2,1,0:T(8,128)(2,1)S(1)}, bf16[2,512,128]{2,1,0:T(8,128)(2,1)S(1)}, u32[]{:S(2)}, u32[]{:S(2)}) collective-permute-start(bf16[2,512,128]{2,1,0:T(8,128)(2,1)S(1)} %shard_map.69.refs_4_), channel_id=1, source_target_pairs={{4,8},{8,4},{5,9},{9,5},{6,10},{10,6},{7,11},{11,7},{20,24},{24,20... | collective-permute-start | bytes 786440 | tf_op jit(solution)/shard_map/ppermute | solution.py:425
  30.3 4.6 %collective-permute-start.9 = (bf16[512,128]{1,0:T(8,128)(2,1)S(1)}, bf16[512,128]{1,0:T(8,128)(2,1)S(1)}, u32[]{:S(2)}, u32[]{:S(2)}) collective-permute-start(bf16[512,128]{1,0:T(8,128)(2,1)S(1)} %get-tuple-element.27), channel_id=1, source_target_pairs={{0,2},{2,0},{1,3},{3,1},{4,6},{6,4},{5,7},{7,5},{8,10},{10,8},{9,1... | collective-permute-start | bytes 393224 | tf_op jit(solution)/shard_map/ppermute | solution.py:414
  30.7 10.8 %collective-permute-start.12 = (bf16[512,128]{1,0:T(8,128)(2,1)S(1)}, bf16[512,128]{1,0:T(8,128)(2,1)S(1)}, u32[]{:S(2)}, u32[]{:S(2)}) collective-permute-start(bf16[512,128]{1,0:T(8,128)(2,1)S(1)} %get-tuple-element.28.piece_ref), channel_id=1, source_target_pairs={{0,1},{1,0},{2,3},{3,2},{4,5},{5,4},{6,7},{7,6},{8,9},{9,8},{10,11... | collective-permute-start | bytes 393224 | tf_op jit(solution)/shard_map/ppermute | solution.py:410
  34.9 7.2 %collective-permute-start.10 = (bf16[512,128]{1,0:T(8,128)(2,1)S(1)}, bf16[512,128]{1,0:T(8,128)(2,1)S(1)}, u32[]{:S(2)}, u32[]{:S(2)}) collective-permute-start(bf16[512,128]{1,0:T(8,128)(2,1)S(1)} %collective-permute-done.9.piece_ref), channel_id=1, source_target_pairs={{0,1},{1,0},{2,3},{3,2},{4,5},{5,4},{6,7},{7,6},{8,9},{9,8},{10,11... | collective-permute-start | bytes 393224 | tf_op jit(solution)/shard_map/ppermute | solution.py:410
